TPU v7x, 512 devices: a whole 4x8x8 slice. The times are simulated.
512 devices in a mesh: ta: 8 (over z), af: 8 (over y_lo, x), sa: 8 (over y_hi, core).
Axes of the slice: x: 4, y: 8 (y_hi: 4, y_lo: 2; y = y_hi * 2 + y_lo), z: 8, core: 2. Of those that a mesh axis runs over, the one named last changes fastest.
Arguments:
- blocks: bfloat16 [8, 8, 8, 4, 64, 4096], P('ta', 'af', 'sa'), may hold values from -6 to 6
- coords: int32 [8, 8, 8, 4, 3], P('ta', 'af', 'sa'), may hold values from 0 to 1, as said below
- counts: int32 [8, 8, 8], P('ta', 'af', 'sa'), may hold values from 1 to 4, as said below
- time_factor: float32 [8, 128, 256], P('ta', ('af', 'sa')), may hold values from -2.4 to 2.4
- freq_factor: float32 [8, 128, 256], P('af', ('ta', 'sa')), may hold values from -2.4 to 2.4
- subj_factor: float32 [8, 128, 256], P('sa', ('ta', 'af')), may hold values from -2.4 to 2.4
- time_velocity: float32 [8, 128, 256], P('ta', ('af', 'sa')), may hold values from -1.8 to 1.8
- freq_velocity: float32 [8, 128, 256], P('af', ('ta', 'sa')), may hold values from -1.8 to 1.8
- subj_velocity: float32 [8, 128, 256], P('sa', ('ta', 'af')), may hold values from -1.8 to 1.8
Outputs:
- new_time: float32 [8, 128, 256], P('ta', ('af', 'sa'))
- new_freq: float32 [8, 128, 256], P('af', ('ta', 'sa'))
- new_subj: float32 [8, 128, 256], P('sa', ('ta', 'af'))
- new_time_velocity: float32 [8, 128, 256], P('ta', ('af', 'sa'))
- new_freq_velocity: float32 [8, 128, 256], P('af', ('ta', 'sa'))
- new_subj_velocity: float32 [8, 128, 256], P('sa', ('ta', 'af'))
Inputs may be any that keep to these rules, and one draw needn't show every extreme that they name: `coords`: entries are 0 or 1; the 4 slots of a device name distinct positions. `counts`: some device has 4 filled slots and some has 1.
All inputs are finite; a program needn't handle non-finite values.
Results may differ from a plain program's by a relative error of at most 0.005.
Values may be sent and summed in bfloat16 or wider, within the bound.
No kernel may reach another device: no remote copies, remote signals or barrier semaphores. Data moves between devices by JAX's collectives and lax.ppermute only.
A program may use at most 64 MiB of HBM per device.

v0:
```python
import jax
import jax.numpy as jnp
from jax import lax
from jax.sharding import PartitionSpec as P

BF = 64
BS = 64


def block_terms(
    block_data, time_table, freq_table, subj_table, position, valid, freq_extent, subj_extent
):
    time_extent = block_data.shape[0]
    time_block = lax.dynamic_slice_in_dim(time_table, position[0] * time_extent, time_extent, 0)
    freq_block = lax.dynamic_slice_in_dim(freq_table, position[1] * freq_extent, freq_extent, 0)
    subj_block = lax.dynamic_slice_in_dim(subj_table, position[2] * subj_extent, subj_extent, 0)
    freq_wide = freq_block.astype(jnp.float32)
    subj_wide = subj_block.astype(jnp.float32)
    khatri = (freq_wide[:, None, :] * subj_wide[None, :, :]).astype(jnp.bfloat16)
    khatri = khatri.reshape(freq_extent * subj_extent, -1)
    approx = lax.dot_general(
        time_block, khatri, (((1,), (1,)), ((), ())), preferred_element_type=jnp.float32
    )
    observed = block_data.astype(jnp.float32)
    misfit = ((approx - observed) * valid).astype(jnp.bfloat16)
    grad_time = jnp.dot(misfit, khatri, preferred_element_type=jnp.float32)
    contracted = lax.dot_general(
        misfit, time_block, (((0,), (0,)), ((), ())), preferred_element_type=jnp.float32
    )
    contracted = contracted.reshape(freq_extent, subj_extent, -1)
    grad_freq = jnp.sum(contracted * subj_wide[None, :, :], axis=1)
    grad_subj = jnp.sum(contracted * freq_wide[:, None, :], axis=0)
    return (grad_time, grad_freq, grad_subj)


def add_rows(accumulated, block_grad, offset):
    current = lax.dynamic_slice_in_dim(accumulated, offset, block_grad.shape[0], 0)
    return lax.dynamic_update_slice_in_dim(accumulated, current + block_grad, offset, 0)


def per_device(
    blocks,
    coords,
    counts,
    time_factor,
    freq_factor,
    subj_factor,
    time_velocity,
    freq_velocity,
    subj_velocity,
):
    time_table = lax.all_gather(time_factor.astype(jnp.bfloat16), ("af", "sa"), axis=1, tiled=True)[
        0
    ]
    freq_table = lax.all_gather(freq_factor.astype(jnp.bfloat16), ("ta", "sa"), axis=1, tiled=True)[
        0
    ]
    subj_table = lax.all_gather(subj_factor.astype(jnp.bfloat16), ("ta", "af"), axis=1, tiled=True)[
        0
    ]
    local_blocks = blocks[0, 0, 0]
    local_coords = coords[0, 0, 0]
    filled = counts[0, 0, 0]
    time_extent = local_blocks.shape[1]
    freq_extent = BF
    subj_extent = BS

    def visit_slot(slot_index, running, valid):
        position = local_coords[slot_index]
        grad_time, grad_freq, grad_subj = block_terms(
            local_blocks[slot_index],
            time_table,
            freq_table,
            subj_table,
            position,
            valid,
            freq_extent,
            subj_extent,
        )
        return (
            add_rows(running[0], grad_time, position[0] * time_extent),
            add_rows(running[1], grad_freq, position[1] * freq_extent),
            add_rows(running[2], grad_subj, position[2] * subj_extent),
        )

    initial = (
        jnp.zeros(time_table.shape, jnp.float32),
        jnp.zeros(freq_table.shape, jnp.float32),
        jnp.zeros(subj_table.shape, jnp.float32),
    )
    running = lax.fori_loop(
        0,
        local_blocks.shape[0],
        lambda slot_index, running: visit_slot(
            slot_index, running, (slot_index < filled).astype(jnp.float32)
        ),
        initial,
    )
    time_grad = lax.psum_scatter(running[0][None], ("af", "sa"), scatter_dimension=1, tiled=True)
    freq_grad = lax.psum_scatter(running[1][None], ("ta", "sa"), scatter_dimension=1, tiled=True)
    subj_grad = lax.psum_scatter(running[2][None], ("ta", "af"), scatter_dimension=1, tiled=True)
    new_time_velocity = 0.9 * time_velocity + time_grad / 64.0
    new_freq_velocity = 0.9 * freq_velocity + freq_grad / 64.0
    new_subj_velocity = 0.9 * subj_velocity + subj_grad / 64.0
    new_time = time_factor - 0.5 * new_time_velocity
    new_freq = freq_factor - 0.5 * new_freq_velocity
    new_subj = subj_factor - 0.5 * new_subj_velocity
    return (new_time, new_freq, new_subj, new_time_velocity, new_freq_velocity, new_subj_velocity)


def solution(mesh):
    return jax.shard_map(
        per_device,
        mesh=mesh,
        in_specs=(
            P("ta", "af", "sa", None, None, None),
            P("ta", "af", "sa", None, None),
            P("ta", "af", "sa"),
            P("ta", ("af", "sa"), None),
            P("af", ("ta", "sa"), None),
            P("sa", ("ta", "af"), None),
            P("ta", ("af", "sa"), None),
            P("af", ("ta", "sa"), None),
            P("sa", ("ta", "af"), None),
        ),
        out_specs=(
            P("ta", ("af", "sa"), None),
            P("af", ("ta", "sa"), None),
            P("sa", ("ta", "af"), None),
            P("ta", ("af", "sa"), None),
            P("af", ("ta", "sa"), None),
            P("sa", ("ta", "af"), None),
        ),
        check_vma=False,
    )
```

profile of v0, /device:TPU:1, one launch (start us, length us, event | category | flops | bytes accessed | tf_op | source)
XLA Modules:
  0.0 1543.5 jit_solution(18307715518159447462)
XLA Ops:
  7.2 0.0 all-reduce.7.cloned.1.call-start
  7.2 0.8 copy.20
  8.0 0.7 copy.41
  8.7 76.2 %all_gather.9 = bf16[1,128,256]{2,0,1:T(2,128)(2,1)S(1)} all-gather(bf16[1,2,256]{2,0,1:T(2,128)(2,1)S(1)} %copy.41), channel_id=1, replica_groups=mesh['ta'=8,'af'=8,'sa'=8] {'af','sa'}, dimensions={1}, use_global_device_ids=true | all-gather | bytes 66560 | tf_op jit(solution)/shard_map/all_gather | solution.py:52
  84.9 0.7 copy.40
  85.6 83.4 %all_gather.10 = bf16[1,128,256]{2,0,1:T(2,128)(2,1)S(1)} all-gather(bf16[1,2,256]{2,0,1:T(2,128)(2,1)S(1)} %copy.40), channel_id=1, replica_groups=mesh['ta'=8,'af'=8,'sa'=8] {'ta','sa'}, dimensions={1}, use_global_device_ids=true | all-gather | bytes 66560 | tf_op jit(solution)/shard_map/all_gather | solution.py:55
  169.0 0.7 copy.39
  169.7 134.7 %all_gather.11 = bf16[1,128,256]{2,0,1:T(2,128)(2,1)S(1)} all-gather(bf16[1,2,256]{2,0,1:T(2,128)(2,1)S(1)} %copy.39), channel_id=1, replica_groups=mesh['ta'=8,'af'=8,'sa'=8] {'ta','af'}, dimensions={1}, use_global_device_ids=true | all-gather | bytes 66560 | tf_op jit(solution)/shard_map/all_gather | solution.py:58
  304.5 30.4 %while.17 = (s32[]{:T(128)}, f32[128,256]{1,0:T(8,128)S(1)}, f32[128,256]{1,0:T(8,128)S(1)}, f32[128,256]{1,0:T(8,128)S(1)}, s32[4,3]{1,0:T(4,128)S(1)}, /*index...) while((s32[]{:T(128)}, f32[128,256]{1,0:T(8,128)S(1)}, ...), condition=%wide.region_3.0_spmd, body=%wide.region_0.0_spmd.sunk | while | flops 410042368 | bytes 17957244 | solution.py:91
  304.5 0.6 fusion.32
  307.1 0.7 multiply_convert_fusion.2
  308.5 1.8 fusion.33
  310.3 0.5 fusion.34
  310.8 0.8 multiply_reduce_fusion.4
  311.5 0.5 multiply_reduce_fusion.5
  312.1 0.6 fusion.32
  314.7 0.7 multiply_convert_fusion.2
  316.1 1.8 fusion.33
  317.9 0.5 fusion.34
  318.4 0.8 multiply_reduce_fusion.4
  319.1 0.5 multiply_reduce_fusion.5
  319.7 0.6 fusion.32
  322.3 0.7 multiply_convert_fusion.2
  323.7 1.8 fusion.33
  325.5 0.5 fusion.34
  326.0 0.8 multiply_reduce_fusion.4
  326.7 0.5 multiply_reduce_fusion.5
  327.3 0.6 fusion.32
  329.9 0.7 multiply_convert_fusion.2
  331.3 1.8 fusion.33
  333.1 0.5 fusion.34
  333.6 0.8 multiply_reduce_fusion.4
  334.3 0.5 multiply_reduce_fusion.5
  335.0 0.6 copy-done
  335.6 0.0 all-reduce.7.cloned.1.call-update
  335.6 0.0 all-reduce.9.cloned.1.call-start
  335.7 0.7 all-reduce.9.cloned.1.call-update
  336.3 0.0 all-reduce.11.cloned.1.call-start
  336.4 0.7 all-reduce.11.cloned.1.call-update
  337.1 1.3 dynamic-slice
  338.4 1.3 dynamic-slice.2
  340.9 1.3 dynamic-slice.4
  342.8 194.6 %all-reduce.7.cloned.1.call-done = f32[1,128,256]{2,1,0:T(8,128)} async-done(((f32[1,128,256]{2,1,0:T(8,128)}), f32[1,128,256]{2,1,0:T(8,128)}) %all-reduce.7.cloned.1.call-update) | async-done | bytes 131088
  537.4 1.3 multiply_subtract_fusion.2
  538.7 489.6 %all-reduce.9.cloned.1.call-done = f32[1,128,256]{2,1,0:T(8,128)} async-done(((f32[1,128,256]{2,1,0:T(8,128)}), f32[1,128,256]{2,1,0:T(8,128)}) %all-reduce.9.cloned.1.call-update) | async-done | bytes 131088
  1028.3 1.3 multiply_subtract_fusion.1
  1029.6 506.1 %all-reduce.11.cloned.1.call-done = f32[1,128,256]{2,1,0:T(8,128)} async-done(((f32[1,128,256]{2,1,0:T(8,128)}), f32[1,128,256]{2,1,0:T(8,128)}) %all-reduce.11.cloned.1.call-update) | async-done | bytes 131088
  1535.7 1.3 multiply_subtract_fusion
  (39 shorter events, 0.3 us)
Async XLA Ops:
  7.2 530.3 %all-reduce.7.cloned.1.call-start = ((), (), s32[]{:S(2)}) async-start(), calls=%async_computation | async-start | bytes 262144
  304.4 233.0 %copy-start.3 = (f32[1,2,256]{2,1,0:T(2,128)S(1)}, f32[1,2,256]{2,1,0:T(2,128)}, u32[]{:S(2)}) copy-start(f32[1,2,256]{2,1,0:T(2,128)} %param.14) | copy-start | bytes 6148
  304.4 233.0 %copy-start.6 = (f32[1,2,256]{2,1,0:T(2,128)S(1)}, f32[1,2,256]{2,1,0:T(2,128)}, u32[]{:S(2)}) copy-start(f32[1,2,256]{2,1,0:T(2,128)} %param.17) | copy-start | bytes 6148
  304.4 723.9 %copy-start.4 = (f32[1,2,256]{2,1,0:T(2,128)S(1)}, f32[1,2,256]{2,1,0:T(2,128)}, u32[]{:S(2)}) copy-start(f32[1,2,256]{2,1,0:T(2,128)} %param.15) | copy-start | bytes 6148
  304.5 723.9 %copy-start.7 = (f32[1,2,256]{2,1,0:T(2,128)S(1)}, f32[1,2,256]{2,1,0:T(2,128)}, u32[]{:S(2)}) copy-start(f32[1,2,256]{2,1,0:T(2,128)} %param.18) | copy-start | bytes 6148
  304.5 1231.2 %copy-start.5 = (f32[1,2,256]{2,1,0:T(2,128)S(1)}, f32[1,2,256]{2,1,0:T(2,128)}, u32[]{:S(2)}) copy-start(f32[1,2,256]{2,1,0:T(2,128)} %param.16) | copy-start | bytes 6148
  304.5 1231.2 %copy-start.8 = (f32[1,2,256]{2,1,0:T(2,128)S(1)}, f32[1,2,256]{2,1,0:T(2,128)}, u32[]{:S(2)}) copy-start(f32[1,2,256]{2,1,0:T(2,128)} %param.19) | copy-start | bytes 6148
  334.9 0.6 copy-start
  334.9 0.7 copy-start.1
  334.9 1.5 copy-start.2
  335.6 692.7 %all-reduce.9.cloned.1.call-start = ((), (), s32[]{:S(2)}) async-start(), calls=%async_computation.1 | async-start | bytes 262144
  336.3 1199.3 %all-reduce.11.cloned.1.call-start = ((), (), s32[]{:S(2)}) async-start(), calls=%async_computation.2 | async-start | bytes 262144
Sparse Core Ops, SparseCore 0:
  335.7 201.6 all-reduce.6
  540.3 487.9 all-reduce.8
  1031.5 504.1 all-reduce.10
where the time goes:
time: 1570 us; the launch traced here: 1540 us
  waiting for transfers between devices  1190 us (76%)
  blocking collectives  294 us (19%)
  between operations  15.8 us (1%)
    unnamed x6, waiting for transfers between devices  1190 us
    all_gather x1, blocking collectives, per_device(): lax.all_gather(subj_factor.astype(jnp.bfloat16), ('ta', 'af'), axis=1, ti...  135 us
    all_gather x1, blocking collectives, per_device(): lax.all_gather(freq_factor.astype(jnp.bfloat16), ('ta', 'sa'), axis=1, ti...  83.4 us
    all_gather x1, blocking collectives, per_device(): lax.all_gather(time_factor.astype(jnp.bfloat16), ('af', 'sa'), axis=1, ti...  76.2 us
  transfers between devices with their start and end apart: 3, of which 3 were waited for; matrix products, arithmetic and copies ran while one was open for 0% of the time, Pallas kernels for 0%

commit v1 on v0

v1 whole, which is shorter than its diff:
```python
import functools

import jax
import jax.numpy as jnp
from jax import lax
from jax.experimental import pallas as pl
from jax.experimental.pallas import tpu as pltpu
from jax.sharding import PartitionSpec as P

BF16 = jnp.bfloat16
F32 = jnp.float32
ROWS = 2
HALF = 128
SEND = BF16


def put_rows(tile, at, rows):
    tile[at : at + 2, :] = rows[:, :HALF]
    tile[at + 2 : at + 4, :] = rows[:, HALF:]


def pack_factors(n_af, n_sa, time_ref, freq_ref, subj_ref, out_ref, with_freq, with_subj):
    mine = lax.axis_index("af")
    put_rows(with_freq, 0, time_ref[0])
    put_rows(with_subj, 0, time_ref[0])
    put_rows(with_freq, 4, freq_ref[0])
    put_rows(with_subj, 4, subj_ref[0])
    freq_tile = with_freq[...].astype(BF16)
    subj_tile = with_subj[...].astype(BF16)
    out_ref[...] = jnp.broadcast_to(subj_tile[None], out_ref.shape)
    out_ref[pl.ds(mine * n_sa, n_sa)] = jnp.broadcast_to(freq_tile[None], (n_sa, 8, HALF))


def join_factors(n_af, n_sa, got_ref, subj_ref, out_ref, wide, joined):
    af = lax.axis_index("af")
    sa = lax.axis_index("sa")
    slots = n_af * n_sa
    wide[...] = got_ref[...].astype(F32).reshape(slots * 8, HALF)
    own = subj_ref[0].astype(BF16).astype(F32)
    is_own = lax.broadcasted_iota(jnp.int32, (n_af, HALF), 0) == af
    for half in range(2):
        for row in range(ROWS):
            at = 4 + 2 * half + row
            freq = wide[pl.ds(af * (n_sa * 8) + at, n_sa, stride=8), :]
            joined[half, pl.ds(row, n_sa, stride=ROWS), :] = freq
            subj = wide[pl.ds(sa * 8 + at, n_af, stride=n_sa * 8), :]
            mine = own[row : row + 1, half * HALF : (half + 1) * HALF]
            subj = jnp.where(is_own, mine, subj)
            joined[half, pl.ds(ROWS * n_sa + row, n_af, stride=ROWS), :] = subj
    rows = jnp.concatenate([joined[0], joined[1]], axis=1).astype(BF16)
    for peer in range(out_ref.shape[0]):
        out_ref[peer] = rows


def main_body(
    dims,
    coords_ref,
    counts_ref,
    blocks_ref,
    first_ref,
    second_ref,
    pair_ref,
    time_ref,
    wide,
    time_table,
    acc_time,
    acc_freq,
    acc_subj,
):
    n_ta, n_af, n_sa, bt, bf, bs, step = dims
    slot = pl.program_id(0)
    slots = n_af * n_sa

    @pl.when(slot == 0)
    def _():
        wide[...] = first_ref[...].astype(F32).reshape(slots * 8, HALF)
        for half in range(2):
            for row in range(ROWS):
                time_table[half, pl.ds(row, slots, stride=ROWS), :] = wide[
                    pl.ds(2 * half + row, slots, stride=8), :
                ]
        acc_time[...] = jnp.zeros_like(acc_time)
        acc_freq[...] = jnp.zeros_like(acc_freq)
        acc_subj[...] = jnp.zeros_like(acc_subj)

    @pl.when(slot < counts_ref[0, 0, 0])
    def _():
        time_at = pl.multiple_of(coords_ref[0, 0, 0, slot, 0] * bt, bt)
        freq_at = coords_ref[0, 0, 0, slot, 1]
        subj_at = coords_ref[0, 0, 0, slot, 2]
        half_ta = n_ta // 2
        n_freq = ROWS * n_sa
        a = jnp.concatenate(
            [time_table[half, pl.ds(time_at, bt), :].astype(BF16) for half in range(2)], axis=1
        )
        b = second_ref[pl.ds(freq_at * half_ta, half_ta), :n_freq, :].reshape(bf, -1).astype(F32)
        c = second_ref[pl.ds(subj_at * half_ta, half_ta), n_freq:, :].reshape(bs, -1).astype(F32)
        freq_row = pl.multiple_of(freq_at * bf, bf)
        subj_row = pl.multiple_of(subj_at * bs, bs)
        grad_time = jnp.zeros(a.shape, F32)
        grad_subj = jnp.zeros(c.shape, F32)
        for j in range(0, bf, step):
            khatri = (b[j : j + step][:, None, :] * c[None]).astype(BF16).reshape(step * bs, -1)
            approx = lax.dot_general(
                a, khatri, (((1,), (1,)), ((), ())), preferred_element_type=F32
            )
            observed = blocks_ref[0, 0, 0, 0, :, j * bs : (j + step) * bs].astype(F32)
            misfit = (approx - observed).astype(BF16)
            grad_time += jnp.dot(misfit, khatri, preferred_element_type=F32)
            contracted = lax.dot_general(
                misfit, a, (((0,), (0,)), ((), ())), preferred_element_type=F32
            ).reshape(step, bs, -1)
            acc_freq[pl.ds(freq_row + j, step), :] += jnp.sum(contracted * c[None], axis=1)
            for k in range(step):
                grad_subj += contracted[k] * b[j + k : j + k + 1]
        acc_time[pl.ds(time_at, bt), :] += grad_time
        acc_subj[pl.ds(subj_row, bs), :] += grad_subj

    @pl.when(slot == pl.num_programs(0) - 1)
    def _():
        for half in range(2):
            time_ref[half] = acc_time[:, half * HALF : (half + 1) * HALF]
        for t in range(n_ta):
            n_freq, n_subj = ROWS * n_sa, ROWS * n_af
            pair_ref[t, :n_freq, :] = acc_freq[t * n_freq : (t + 1) * n_freq, :].astype(SEND)
            pair_ref[t, n_freq:, :] = acc_subj[t * n_subj : (t + 1) * n_subj, :].astype(SEND)


def pack_grads(n_af, n_sa, got_ref, time_ref, out_ref, own_ref, summed, wide):
    af = lax.axis_index("af")
    slots = n_af * n_sa
    n_freq = ROWS * n_sa
    total = jnp.sum(got_ref[...].astype(F32), axis=0)
    for half in range(2):
        summed[half] = total[:, half * HALF : (half + 1) * HALF]
    for half in range(2):
        for row in range(ROWS):
            wide[pl.ds(2 * half + row, slots, stride=8), :] = time_ref[
                half, pl.ds(row, slots, stride=ROWS), :
            ]
            at = 4 + 2 * half + row
            for peer in range(n_af):
                there = n_freq + ROWS * peer + row
                subj = summed[half, there : there + 1, :]
                wide[pl.ds(peer * n_sa * 8 + at, n_sa, stride=8), :] = jnp.broadcast_to(
                    subj, (n_sa, HALF)
                )
            wide[pl.ds(af * (n_sa * 8) + at, n_sa, stride=8), :] = summed[
                half, pl.ds(row, n_sa, stride=ROWS), :
            ]
        own_ref[:, half * HALF : (half + 1) * HALF] = summed[
            half, pl.ds(n_freq + ROWS * af, ROWS), :
        ]
    out_ref[...] = wide[...].astype(SEND).reshape(slots, 8, HALF)


def update(
    n_af,
    n_sa,
    got_ref,
    own_ref,
    time_ref,
    freq_ref,
    subj_ref,
    time_vel_ref,
    freq_vel_ref,
    subj_vel_ref,
    new_time_ref,
    new_freq_ref,
    new_subj_ref,
    new_time_vel_ref,
    new_freq_vel_ref,
    new_subj_vel_ref,
):
    af = lax.axis_index("af")
    sa = lax.axis_index("sa")
    time = jnp.sum(got_ref[...].astype(F32), axis=0)
    freq = jnp.sum(got_ref[pl.ds(af * n_sa, n_sa)].astype(F32), axis=0)
    subj = jnp.zeros_like(freq)
    for peer in range(n_af):
        there = got_ref[peer * n_sa + sa].astype(F32)
        subj += jnp.where(peer == af, jnp.zeros_like(there), there)
    own = own_ref[...]
    for half in range(2):
        lanes = slice(half * HALF, (half + 1) * HALF)
        rows = slice(2 * half, 2 * half + 2)
        more = slice(4 + 2 * half, 6 + 2 * half)
        for grad, old, vel, new, new_vel in (
            (time[rows], time_ref, time_vel_ref, new_time_ref, new_time_vel_ref),
            (freq[more], freq_ref, freq_vel_ref, new_freq_ref, new_freq_vel_ref),
            (subj[more] + own[:, lanes], subj_ref, subj_vel_ref, new_subj_ref, new_subj_vel_ref),
        ):
            velocity = 0.9 * vel[0, :, lanes] + grad / 64.0
            new_vel[0, :, lanes] = velocity
            new[0, :, lanes] = old[0, :, lanes] - 0.5 * velocity


def per_device(sizes, *args):
    n_ta, n_af, n_sa = sizes
    blocks, coords, counts, time, freq, subj, time_vel, freq_vel, subj_vel = args
    slots = n_af * n_sa
    cap, bt = blocks.shape[3:5]
    rank = time.shape[-1]
    bf = ROWS * n_ta * n_sa // 2
    bs = ROWS * n_ta * n_af // 2
    pair_rows = ROWS * (n_sa + n_af)
    tile = jax.ShapeDtypeStruct((slots, 8, HALF), BF16)

    packed = pl.pallas_call(
        functools.partial(pack_factors, n_af, n_sa),
        out_shape=tile,
        scratch_shapes=[pltpu.VMEM((8, HALF), F32)] * 2,
        name="pack_factors",
    )(time, freq, subj)
    first = lax.all_to_all(packed, ("af", "sa"), 0, 0, tiled=True)
    joined = pl.pallas_call(
        functools.partial(join_factors, n_af, n_sa),
        out_shape=jax.ShapeDtypeStruct((n_ta, pair_rows, rank), BF16),
        scratch_shapes=[pltpu.VMEM((slots * 8, HALF), F32), pltpu.VMEM((2, pair_rows, HALF), F32)],
        name="join_factors",
    )(first, subj)
    second = lax.all_to_all(joined, "ta", 0, 0, tiled=True)

    table = (ROWS * slots, rank)
    halves = (2, ROWS * slots, HALF)
    step = min(8, bf)
    dims = (n_ta, n_af, n_sa, bt, bf, bs, step)
    pair, time_grad = pl.pallas_call(
        functools.partial(main_body, dims),
        grid=(cap,),
        in_specs=[
            pl.BlockSpec(memory_space=pltpu.SMEM),
            pl.BlockSpec(memory_space=pltpu.SMEM),
            pl.BlockSpec((1, 1, 1, 1, bt, bf * bs), lambda i: (0, 0, 0, i, 0, 0)),
            pl.BlockSpec((slots, 8, HALF), lambda i: (0, 0, 0)),
            pl.BlockSpec((n_ta, pair_rows, rank), lambda i: (0, 0, 0)),
        ],
        out_specs=[
            pl.BlockSpec((n_ta, pair_rows, rank), lambda i: (0, 0, 0)),
            pl.BlockSpec(halves, lambda i: (0, 0, 0)),
        ],
        out_shape=[
            jax.ShapeDtypeStruct((n_ta, pair_rows, rank), SEND),
            jax.ShapeDtypeStruct(halves, F32),
        ],
        scratch_shapes=[
            pltpu.VMEM((slots * 8, HALF), F32),
            pltpu.VMEM(halves, F32),
            pltpu.VMEM(table, F32),
            pltpu.VMEM((2 * bf, rank), F32),
            pltpu.VMEM((2 * bs, rank), F32),
        ],
        compiler_params=pltpu.CompilerParams(
            dimension_semantics=("arbitrary",), vmem_limit_bytes=32 << 20
        ),
        name="block_grads",
    )(coords, counts, blocks, first, second)

    third = lax.all_to_all(pair, "ta", 0, 0, tiled=True)
    packed_grads, own = pl.pallas_call(
        functools.partial(pack_grads, n_af, n_sa),
        out_shape=[
            jax.ShapeDtypeStruct((slots, 8, HALF), SEND),
            jax.ShapeDtypeStruct((ROWS, rank), F32),
        ],
        scratch_shapes=[
            pltpu.VMEM((2, pair_rows, HALF), F32),
            pltpu.VMEM((slots * 8, HALF), F32),
        ],
        name="pack_grads",
    )(third, time_grad)
    fourth = lax.all_to_all(packed_grads, ("af", "sa"), 0, 0, tiled=True)
    return pl.pallas_call(
        functools.partial(update, n_af, n_sa),
        out_shape=[jax.ShapeDtypeStruct(time.shape, F32)] * 6,
        name="update",
    )(fourth, own, time, freq, subj, time_vel, freq_vel, subj_vel)


def solution(mesh):
    sizes = tuple(mesh.shape[name] for name in ("ta", "af", "sa"))
    factors = (P("ta", ("af", "sa"), None), P("af", ("ta", "sa"), None), P("sa", ("ta", "af"), None))
    return jax.shard_map(
        lambda *args: tuple(per_device(sizes, *args)),
        mesh=mesh,
        in_specs=(
            P("ta", "af", "sa", None, None, None),
            P("ta", "af", "sa", None, None),
            P("ta", "af", "sa"),
            *factors,
            *factors,
        ),
        out_specs=(*factors, *factors),
        check_vma=False,
    )
```

time: 1570 us -> 90.6 us (0.06); the launches traced: 1540 us -> 90 us
  waiting for transfers between devices: 1190 us -> 6.51 us
  blocking collectives: 294 us -> 56.1 us
    unnamed x6 -> x0, waiting for transfers between devices: 1190 us -> none
    all_gather x3 -> x0, blocking collectives: 294 us -> none  [the longest x1 135 us: per_device(): lax.all_gather(subj_factor.astype(jnp.bfloat16), ('ta', 'af'), axis=1, ti...]
    all_to_all x0 -> x3, blocking collectives: none -> 56.1 us  [the longest x1 22.1 us: per_device(): first = lax.all_to_all(packed, ('af', 'sa'), 0, 0, tiled=True)]
  transfers between devices with their start and end apart: 3 -> 1, of which waited for: 3 -> 1; matrix products, arithmetic and copies ran while one was open for 0% -> 1% of each run, Pallas kernels for 0% -> 0%
where the time goes in v1:
time: 90.6 us; the launch traced here: 90 us
  blocking collectives  56.1 us (62%)
  Pallas kernels  12.2 us (13%)
  starting transfers between devices  10.1 us (11%)
  waiting for transfers between devices  6.51 us (7%)
  local copies, waits for them, and re-layouts  3.91 us (4%)
  between operations  1.31 us (1%)
    all_to_all x1, blocking collectives, per_device(): first = lax.all_to_all(packed, ('af', 'sa'), 0, 0, tiled=True)  22.1 us
    all_to_all x1, blocking collectives, per_device(): fourth = lax.all_to_all(packed_grads, ('af', 'sa'), 0, 0, tiled=True)  18.4 us
    all_to_all x1, blocking collectives, per_device(): third = lax.all_to_all(pair, 'ta', 0, 0, tiled=True)  15.6 us
    all_to_all x1, starting transfers between devices, per_device(): second = lax.all_to_all(joined, 'ta', 0, 0, tiled=True)  10.1 us
    all_to_all x1, waiting for transfers between devices, per_device(): second = lax.all_to_all(joined, 'ta', 0, 0, tiled=True)  6.51 us
    pallas_call x1, Pallas kernels, per_device(): pl.pallas_call(functools.partial(main_body, dims), grid=(cap,), in_specs=...  5.87 us
    unnamed x7, local copies, waits for them, and re-layouts  3.91 us
  transfers between devices with their start and end apart: 1, of which 1 were waited for; matrix products, arithmetic and copies ran while one was open for 1% of the time, Pallas kernels for 0%

profile of v1, /device:TPU:1, one launch (start us, length us, event | category | flops | bytes accessed | tf_op | source)
XLA Modules:
  0.0 90.0 jit_solution(1606369058183168958)
XLA Ops:
  0.6 1.4 %pack_factors.1 = bf16[64,8,128]{2,1,0:T(8,128)(2,1)} custom-call(f32[1,2,256]{2,1,0:T(2,128)} %time_ref.3, f32[1,2,256]{2,1,0:T(2,128)} %freq_ref.3, f32[1,2,256]{2,1,0:T(2,128)} %subj_ref.5), custom_call_target="tpu_custom_call" | custom-call | tf_op jit(solution)/shard_map/pack_factors/pallas_call | solution.py:209
  2.0 22.1 %all_to_all.20.got_ref.first_ref = bf16[64,8,128]{2,1,0:T(8,128)(2,1)} all-to-all(bf16[64,8,128]{2,1,0:T(8,128)(2,1)} %pack_factors.1), channel_id=1, replica_groups=mesh['ta'=8,'af'=8,'sa'=8] {'af','sa'}, dimensions={0} | all-to-all | bytes 262144 | tf_op jit(solution)/shard_map/all_to_all | solution.py:215
  24.1 1.6 %join_factors.1 = bf16[8,32,256]{2,1,0:T(8,128)(2,1)} custom-call(bf16[64,8,128]{2,1,0:T(8,128)(2,1)} %all_to_all.20.got_ref.first_ref, f32[1,2,256]{2,1,0:T(2,128)} %subj_ref.5), custom_call_target="tpu_custom_call" | custom-call | tf_op jit(solution)/shard_map/join_factors/pallas_call | solution.py:216
  25.7 10.1 %all-to-all-start.1 = ((bf16[8,32,256]{2,1,0:T(8,128)(2,1)}), bf16[8,32,256]{2,1,0:T(8,128)(2,1)S(1)}, u32[]{:S(2)}, u32[]{:S(2)}) async-start(bf16[8,32,256]{2,1,0:T(8,128)(2,1)} %join_factors.1), calls=%async_computation.1 | async-start | bytes 262144 | tf_op jit(solution)/shard_map/all_to_all | solution.py:222
  36.4 0.8 copy.15.coords_ref
  37.2 6.5 %all-to-all-done.1.second_ref = bf16[8,32,256]{2,1,0:T(8,128)(2,1)S(1)} async-done(((bf16[8,32,256]{2,1,0:T(8,128)(2,1)}), bf16[8,32,256]{2,1,0:T(8,128)(2,1)S(1)}, u32[]{:S(2)}, u32[]{:S(2)}) %all-to-all-start.1) | async-done | bytes 131104 | tf_op jit(solution)/shard_map/all_to_all | solution.py:222
  43.7 0.0 copy-start
  43.7 1.6 %copy-done = bf16[1,1,1,4,64,4096]{5,4,3,2,1,0:T(8,128)(2,1)S(1)} copy-done((bf16[1,1,1,4,64,4096]{5,4,3,2,1,0:T(8,128)(2,1)S(1)}, bf16[1,1,1,4,64,4096]{5,4,3,2,1,0:T(8,128)(2,1)}, u32[]{:S(2)}) %copy-start) | copy-done | bytes 2097176
  45.3 0.0 copy-start.1
  45.3 0.9 %copy-done.1 = bf16[64,8,128]{2,1,0:T(8,128)(2,1)S(1)} copy-done((bf16[64,8,128]{2,1,0:T(8,128)(2,1)S(1)}, bf16[64,8,128]{2,1,0:T(8,128)(2,1)}, u32[]{:S(2)}) %copy-start.1) | copy-done | bytes 131096
  46.2 5.9 %block_grads.1 = (bf16[8,32,256]{2,1,0:T(8,128)(2,1)S(1)}, f32[2,128,128]{2,1,0:T(8,128)S(1)}) custom-call(s32[1,1,1,4,3]{4,3,2,1,0:T(4,128)S(1)} %copy.15.coords_ref, s32[1,1,1]{2,1,0:T(1,128)S(6)} %copy.16.counts_ref, bf16[1,1,1,4,64,4096]{5,4,3,2,1,0:T(8,128)(2,1)S(1)} %copy-done, bf16[64,8,128]{2,1,0:T(8,128)(2,1)S(1)} %copy-done.1, ...), custom_call_target="tpu_custom_call" | custom-call | tf_op jit(solution)/shard_map/block_grads/pallas_call | solution.py:228
  52.0 0.0 copy-start.2
  52.1 0.6 copy-done.2
  52.7 15.6 %all_to_all.21.got_ref = bf16[8,32,256]{2,1,0:T(8,128)(2,1)} all-to-all(bf16[8,32,256]{2,1,0:T(8,128)(2,1)S(1)} %get-tuple-element.10), channel_id=1, replica_groups=mesh['ta'=8,'af'=8,'sa'=8] {'ta'}, dimensions={0} | all-to-all | bytes 262144 | tf_op jit(solution)/shard_map/all_to_all | solution.py:259
  68.3 1.7 %pack_grads.1 = (bf16[64,8,128]{2,1,0:T(8,128)(2,1)}, f32[2,256]{1,0:T(2,128)}) custom-call(bf16[8,32,256]{2,1,0:T(8,128)(2,1)} %all_to_all.21.got_ref, f32[2,128,128]{2,1,0:T(8,128)} %copy-done.2), custom_call_target="tpu_custom_call" | custom-call | tf_op jit(solution)/shard_map/pack_grads/pallas_call | solution.py:260
  70.0 18.4 %all_to_all.22.got_ref = bf16[64,8,128]{2,1,0:T(8,128)(2,1)} all-to-all(bf16[64,8,128]{2,1,0:T(8,128)(2,1)} %get-tuple-element.12), channel_id=1, replica_groups=mesh['ta'=8,'af'=8,'sa'=8] {'af','sa'}, dimensions={0} | all-to-all | bytes 262144 | tf_op jit(solution)/shard_map/all_to_all | solution.py:272
  88.4 1.6 %update.1 = (f32[1,2,256]{2,1,0:T(2,128)}, f32[1,2,256]{2,1,0:T(2,128)}, f32[1,2,256]{2,1,0:T(2,128)}, f32[1,2,256]{2,1,0:T(2,128)}, f32[1,2,256]{2,1,0:T(2,128)}, /*index=5*/f32[1,2,256]{2,1,0:T(2,128)}) custom-call(bf16[64,8,128]{2,1,0:T(8,128)(2,1)} %all_to_all.22.got_ref, f32[2,256]{1,0:T(2,128)} %get-tuple-element.13.own_ref, f32[1,2,256]{2,1,0:T(2,128)} %time_ref.3, ...), custom_call_target="tpu_custom_call" | custom-call | tf_op jit(solution)/shard_map/update/pallas_call | solution.py:273
Async XLA Ops:
  25.7 18.0 %all-to-all-start.1 = ((bf16[8,32,256]{2,1,0:T(8,128)(2,1)}), bf16[8,32,256]{2,1,0:T(8,128)(2,1)S(1)}, u32[]{:S(2)}, u32[]{:S(2)}) async-start(bf16[8,32,256]{2,1,0:T(8,128)(2,1)} %join_factors.1), calls=%async_computation.1 | async-start | bytes 262144 | tf_op jit(solution)/shard_map/all_to_all | solution.py:222
  43.7 1.6 %copy-start = (bf16[1,1,1,4,64,4096]{5,4,3,2,1,0:T(8,128)(2,1)S(1)}, bf16[1,1,1,4,64,4096]{5,4,3,2,1,0:T(8,128)(2,1)}, u32[]{:S(2)}) copy-start(bf16[1,1,1,4,64,4096]{5,4,3,2,1,0:T(8,128)(2,1)} %blocks_ref.1) | copy-start | bytes 6291460
  45.3 0.9 %copy-start.1 = (bf16[64,8,128]{2,1,0:T(8,128)(2,1)S(1)}, bf16[64,8,128]{2,1,0:T(8,128)(2,1)}, u32[]{:S(2)}) copy-start(bf16[64,8,128]{2,1,0:T(8,128)(2,1)} %all_to_all.20.got_ref.first_ref) | copy-start | bytes 393220
  52.0 0.7 copy-start.2

commit v2 on v1

v2 whole, which is shorter than its diff:
```python
import functools

import jax
import jax.numpy as jnp
from jax import lax
from jax.experimental import pallas as pl
from jax.experimental.pallas import tpu as pltpu
from jax.sharding import PartitionSpec as P

BF16 = jnp.bfloat16
F32 = jnp.float32
ROWS = 2
HALF = 128
BIG = 56 * 1000 * 1000
SMALL = 4 << 20
SEND = BF16


def put_rows(tile, at, rows):
    tile[at : at + 2, :] = rows[:, :HALF]
    tile[at + 2 : at + 4, :] = rows[:, HALF:]


def pack_factors(n_sa, own_ref, out_ref, with_freq, with_subj):
    mine = lax.axis_index("af")
    put_rows(with_freq, 0, own_ref[0])
    put_rows(with_subj, 0, own_ref[0])
    put_rows(with_freq, 4, own_ref[1])
    put_rows(with_subj, 4, own_ref[2])
    freq_tile = with_freq[...].astype(BF16)
    subj_tile = with_subj[...].astype(BF16)
    out_ref[...] = jnp.broadcast_to(subj_tile[None], out_ref.shape)
    out_ref[pl.ds(mine * n_sa, n_sa)] = jnp.broadcast_to(freq_tile[None], (n_sa, 8, HALF))


def join_factors(n_af, n_sa, got_ref, packed_ref, out_ref, time_ref, wide, joined, time_table):
    af = lax.axis_index("af")
    sa = lax.axis_index("sa")
    slots = n_af * n_sa
    wide[...] = got_ref[...].astype(F32).reshape(slots * 8, HALF)
    own = packed_ref[jnp.where(af == 0, n_sa, 0)].astype(F32)
    is_own = lax.broadcasted_iota(jnp.int32, (n_af, HALF), 0) == af
    for half in range(2):
        for row in range(ROWS):
            at = 4 + 2 * half + row
            freq = wide[pl.ds(af * (n_sa * 8) + at, n_sa, stride=8), :]
            joined[half, pl.ds(row, n_sa, stride=ROWS), :] = freq
            subj = wide[pl.ds(sa * 8 + at, n_af, stride=n_sa * 8), :]
            subj = jnp.where(is_own, own[at : at + 1], subj)
            joined[half, pl.ds(ROWS * n_sa + row, n_af, stride=ROWS), :] = subj
    rows = jnp.concatenate([joined[0], joined[1]], axis=1).astype(BF16)
    for peer in range(out_ref.shape[0]):
        out_ref[peer] = rows
    for half in range(2):
        for row in range(ROWS):
            time_table[half, pl.ds(row, slots, stride=ROWS), :] = wide[
                pl.ds(2 * half + row, slots, stride=8), :
            ]
    time_ref[...] = jnp.concatenate([time_table[0], time_table[1]], axis=1).astype(BF16)


def dot(a, b, contract=((1,), (0,))):
    return lax.dot_general(a, b, (contract, ((), ())), preferred_element_type=F32)


def gram(table):
    return dot(table, table, ((0,), (0,)))


def model_part(rows, grams):
    high = grams.astype(BF16)
    low = (grams - high.astype(F32)).astype(BF16)
    return dot(rows, high) + dot(rows, low)


def take(ref, which, extent):
    return ref[pl.ds(pl.multiple_of(which * extent, extent), extent), :]


def pair_blocks(ref, freq_at, subj_at, n_freq):
    half_ta = ref.shape[0] // 2
    rank = ref.shape[2]
    freq = ref[pl.ds(freq_at * half_ta, half_ta), :n_freq, :]
    subj = ref[pl.ds(subj_at * half_ta, half_ta), n_freq:, :]
    return freq.reshape(-1, rank), subj.reshape(-1, rank)


def fetch_blocks(blocks_ref, data, sems):
    copies = [
        pltpu.make_async_copy(blocks_ref.at[0, 0, 0, slot], data.at[slot], sems.at[slot])
        for slot in range(data.shape[0])
    ]
    for copy in copies:
        copy.start()
    return copies


def pair_body(
    n_freq,
    where_ref,
    blocks_ref,
    time_ref,
    second_ref,
    pair_ref,
    data,
    grams,
    freq,
    subj,
    sems,
):
    copies = fetch_blocks(blocks_ref, data, sems)
    n_ta = second_ref.shape[0]
    bf = freq.shape[0] // 2
    bs = subj.shape[0] // 2
    bt = time_ref.shape[0] // 2
    n_subj = second_ref.shape[1] - n_freq
    freq[...] = jnp.zeros_like(freq)
    subj[...] = jnp.zeros_like(subj)
    for which in range(2):
        b, c = pair_blocks(second_ref, which, which, n_freq)
        grams[which] = gram(take(time_ref, which, bt))
        grams[2 + which] = gram(b)
        grams[4 + which] = gram(c)
    step = min(8, bf)
    for slot, copy in enumerate(copies):
        copy.wait()

        @pl.when(slot < where_ref[3, slot])
        def _(slot=slot):
            time_at = where_ref[0, slot]
            freq_at = where_ref[1, slot]
            subj_at = where_ref[2, slot]
            a = take(time_ref, time_at, bt)
            b, c = pair_blocks(second_ref, freq_at, subj_at, n_freq)
            time_gram = grams[time_at]
            freq_model = model_part(b, time_gram * grams[4 + subj_at])
            subj_model = model_part(c, time_gram * grams[2 + freq_at])
            wide_b, wide_c = b.astype(F32), c.astype(F32)
            freq_data = []
            subj_data = jnp.zeros(wide_c.shape, F32)
            for j in range(0, bf, step):
                cells = data[slot, :, j * bs : (j + step) * bs]
                cube = dot(cells, a, ((0,), (0,))).reshape(step, bs, -1)
                freq_data.append(jnp.sum(cube * wide_c[None], axis=1))
                for k in range(step):
                    subj_data += cube[k] * wide_b[j + k : j + k + 1]
            freq_data = jnp.concatenate(freq_data, axis=0)
            freq[pl.ds(pl.multiple_of(freq_at * bf, bf), bf), :] += freq_model - freq_data
            subj[pl.ds(pl.multiple_of(subj_at * bs, bs), bs), :] += subj_model - subj_data

    for t in range(n_ta):
        pair_ref[t, :n_freq, :] = freq[t * n_freq : (t + 1) * n_freq, :].astype(SEND)
        pair_ref[t, n_freq:, :] = subj[t * n_subj : (t + 1) * n_subj, :].astype(SEND)


def time_body(
    n_freq, where_ref, blocks_ref, time_ref, second_ref, out_ref, data, grad, sems
):
    copies = fetch_blocks(blocks_ref, data, sems)
    bt = data.shape[1]
    grad[...] = jnp.zeros_like(grad)
    for slot, copy in enumerate(copies):
        copy.wait()

        @pl.when(slot < where_ref[3, slot])
        def _(slot=slot):
            time_at = where_ref[0, slot]
            a = take(time_ref, time_at, bt)
            b, c = pair_blocks(
                second_ref, where_ref[1, slot], where_ref[2, slot], n_freq
            )
            bf, bs = b.shape[0], c.shape[0]
            total = model_part(a, gram(b) * gram(c))
            wide_b = b.astype(F32)
            zero = jnp.zeros_like(c)
            both = jnp.concatenate(
                [jnp.concatenate([c, zero], axis=1), jnp.concatenate([zero, c], axis=1)], axis=0
            )
            rank = c.shape[1]
            for j in range(0, bf, 2):
                part = dot(data[slot, :, j * bs : (j + 2) * bs], both)
                total -= part[:, :rank] * wide_b[j : j + 1]
                total -= part[:, rank:] * wide_b[j + 1 : j + 2]
            grad[pl.ds(pl.multiple_of(time_at * bt, bt), bt), :] += total

    for half in range(2):
        out_ref[half] = grad[:, half * HALF : (half + 1) * HALF]


def kernel_call(body, out_shape, in_spaces, scratch, name, cost, limit):
    return pl.pallas_call(
        body,
        out_shape=out_shape,
        in_specs=[pl.BlockSpec(memory_space=space) for space in in_spaces],
        out_specs=jax.tree.map(lambda _: pl.BlockSpec(memory_space=pltpu.VMEM), out_shape),
        scratch_shapes=scratch,
        compiler_params=pltpu.CompilerParams(vmem_limit_bytes=limit),
        cost_estimate=pl.CostEstimate(flops=cost, bytes_accessed=cost // 200, transcendentals=0),
        name=name,
    )


def pair_grads(n_freq, n_subj, slots_of, blocks, time_table, second):
    cap, bt, cells = blocks.shape[3:]
    n_ta, rows, rank = second.shape
    return kernel_call(
        functools.partial(pair_body, n_freq),
        jax.ShapeDtypeStruct(second.shape, SEND),
        [pltpu.SMEM, pltpu.HBM, pltpu.VMEM, pltpu.VMEM],
        [
            pltpu.VMEM((cap, bt, cells), BF16),
            pltpu.VMEM((6, rank, rank), F32),
            pltpu.VMEM((n_ta * n_freq, rank), F32),
            pltpu.VMEM((n_ta * n_subj, rank), F32),
            pltpu.SemaphoreType.DMA((cap,)),
        ],
        "pair_grads",
        2 * cap * bt * cells * rank,
        BIG,
    )(slots_of, blocks, time_table, second)


def time_grads(n_freq, slots_of, blocks, time_table, second):
    cap, bt, cells = blocks.shape[3:]
    rank = time_table.shape[1]
    return kernel_call(
        functools.partial(time_body, n_freq),
        jax.ShapeDtypeStruct((2, time_table.shape[0], HALF), F32),
        [pltpu.SMEM, pltpu.HBM, pltpu.VMEM, pltpu.VMEM],
        [
            pltpu.VMEM((cap, bt, cells), BF16),
            pltpu.VMEM(time_table.shape, F32),
            pltpu.SemaphoreType.DMA((cap,)),
        ],
        "time_grads",
        2 * cap * bt * cells * rank,
        BIG,
    )(slots_of, blocks, time_table, second)


def pack_grads(n_af, n_sa, got_ref, time_ref, out_ref, own_ref, summed, wide):
    af = lax.axis_index("af")
    slots = n_af * n_sa
    n_freq = ROWS * n_sa
    total = jnp.sum(got_ref[...].astype(F32), axis=0)
    for half in range(2):
        summed[half] = total[:, half * HALF : (half + 1) * HALF]
    for half in range(2):
        for row in range(ROWS):
            wide[pl.ds(2 * half + row, slots, stride=8), :] = time_ref[
                half, pl.ds(row, slots, stride=ROWS), :
            ]
            at = 4 + 2 * half + row
            for peer in range(n_af):
                there = n_freq + ROWS * peer + row
                subj = summed[half, there : there + 1, :]
                wide[pl.ds(peer * n_sa * 8 + at, n_sa, stride=8), :] = jnp.broadcast_to(
                    subj, (n_sa, HALF)
                )
            wide[pl.ds(af * (n_sa * 8) + at, n_sa, stride=8), :] = summed[
                half, pl.ds(row, n_sa, stride=ROWS), :
            ]
        own_ref[:, half * HALF : (half + 1) * HALF] = summed[
            half, pl.ds(n_freq + ROWS * af, ROWS), :
        ]
    out_ref[...] = wide[...].astype(SEND).reshape(slots, 8, HALF)


def update(
    n_af,
    n_sa,
    got_ref,
    own_ref,
    time_ref,
    freq_ref,
    subj_ref,
    time_vel_ref,
    freq_vel_ref,
    subj_vel_ref,
    new_time_ref,
    new_freq_ref,
    new_subj_ref,
    new_time_vel_ref,
    new_freq_vel_ref,
    new_subj_vel_ref,
):
    af = lax.axis_index("af")
    sa = lax.axis_index("sa")
    time = jnp.sum(got_ref[...].astype(F32), axis=0)
    freq = jnp.sum(got_ref[pl.ds(af * n_sa, n_sa)].astype(F32), axis=0)
    subj = jnp.zeros_like(freq)
    for peer in range(n_af):
        there = got_ref[peer * n_sa + sa].astype(F32)
        subj += jnp.where(peer == af, jnp.zeros_like(there), there)
    own = own_ref[...]
    for half in range(2):
        lanes = slice(half * HALF, (half + 1) * HALF)
        rows = slice(2 * half, 2 * half + 2)
        more = slice(4 + 2 * half, 6 + 2 * half)
        for grad, old, vel, new, new_vel in (
            (time[rows], time_ref, time_vel_ref, new_time_ref, new_time_vel_ref),
            (freq[more], freq_ref, freq_vel_ref, new_freq_ref, new_freq_vel_ref),
            (subj[more] + own[:, lanes], subj_ref, subj_vel_ref, new_subj_ref, new_subj_vel_ref),
        ):
            velocity = 0.9 * vel[0, :, lanes] + grad / 64.0
            new_vel[0, :, lanes] = velocity
            new[0, :, lanes] = old[0, :, lanes] - 0.5 * velocity


def per_device(sizes, *args):
    n_ta, n_af, n_sa = sizes
    blocks, coords, counts, time, freq, subj, time_vel, freq_vel, subj_vel = args
    slots = n_af * n_sa
    rank = time.shape[-1]
    pair_rows = ROWS * (n_sa + n_af)
    table = ROWS * slots
    coords = coords.transpose(0, 1, 2, 4, 3).reshape(3, -1)
    slots_of = jnp.concatenate([coords, jnp.broadcast_to(counts.reshape(1, 1), (1, coords.shape[1]))])

    packed = pl.pallas_call(
        functools.partial(pack_factors, n_sa),
        out_shape=jax.ShapeDtypeStruct((slots, 8, HALF), BF16),
        scratch_shapes=[pltpu.VMEM((8, HALF), F32)] * 2,
        compiler_params=pltpu.CompilerParams(vmem_limit_bytes=SMALL),
        name="pack_factors",
    )(jnp.concatenate([time, freq, subj], axis=0))
    first = lax.all_to_all(packed, ("af", "sa"), 0, 0, tiled=True)
    joined, time_table = pl.pallas_call(
        functools.partial(join_factors, n_af, n_sa),
        out_shape=[
            jax.ShapeDtypeStruct((n_ta, pair_rows, rank), BF16),
            jax.ShapeDtypeStruct((table, rank), BF16),
        ],
        scratch_shapes=[
            pltpu.VMEM((slots * 8, HALF), F32),
            pltpu.VMEM((2, pair_rows, HALF), F32),
            pltpu.VMEM((2, table, HALF), F32),
        ],
        compiler_params=pltpu.CompilerParams(vmem_limit_bytes=SMALL),
        name="join_factors",
    )(first, packed)
    second = lax.all_to_all(joined, "ta", 0, 0, tiled=True)
    pair = pair_grads(ROWS * n_sa, ROWS * n_af, slots_of, blocks, time_table, second)
    time_grad = time_grads(ROWS * n_sa, slots_of, blocks, time_table, second)
    third = lax.all_to_all(pair, "ta", 0, 0, tiled=True)
    packed_grads, own = pl.pallas_call(
        functools.partial(pack_grads, n_af, n_sa),
        out_shape=[
            jax.ShapeDtypeStruct((slots, 8, HALF), SEND),
            jax.ShapeDtypeStruct((ROWS, rank), F32),
        ],
        scratch_shapes=[
            pltpu.VMEM((2, pair_rows, HALF), F32),
            pltpu.VMEM((slots * 8, HALF), F32),
        ],
        compiler_params=pltpu.CompilerParams(vmem_limit_bytes=SMALL),
        name="pack_grads",
    )(third, time_grad)
    fourth = lax.all_to_all(packed_grads, ("af", "sa"), 0, 0, tiled=True)
    return pl.pallas_call(
        functools.partial(update, n_af, n_sa),
        out_shape=[jax.ShapeDtypeStruct(time.shape, F32)] * 6,
        compiler_params=pltpu.CompilerParams(vmem_limit_bytes=SMALL),
        name="update",
    )(fourth, own, time, freq, subj, time_vel, freq_vel, subj_vel)


def solution(mesh):
    sizes = tuple(mesh.shape[name] for name in ("ta", "af", "sa"))
    factors = (P("ta", ("af", "sa"), None), P("af", ("ta", "sa"), None), P("sa", ("ta", "af"), None))
    return jax.shard_map(
        lambda *args: tuple(per_device(sizes, *args)),
        mesh=mesh,
        in_specs=(
            P("ta", "af", "sa", None, None, None),
            P("ta", "af", "sa", None, None),
            P("ta", "af", "sa"),
            *factors,
            *factors,
        ),
        out_specs=(*factors, *factors),
        check_vma=False,
    )
```

time: 90.6 us -> 78.7 us (0.87)
  blocking collectives: 56.1 us -> 39.4 us
  starting transfers between devices: 10.1 us -> 13.5 us
  local copies, waits for them, and re-layouts: 3.91 us -> 0.72 us
  waiting for transfers between devices: 6.51 us -> 8.79 us
  Pallas kernels: 12.2 us -> 13.6 us
    all_to_all x1 -> x0, blocking collectives: 15.6 us -> none  [per_device(): third = lax.all_to_all(pair, 'ta', 0, 0, tiled=True)]
    pallas_call x3 -> x4, Pallas kernels: 8.87 us -> 12.9 us  [the longest x1 6.51 us: pair_grads(): kernel_call(functools.partial(pair_body, n_freq), jax.ShapeDtypeStruct(se...]
    all_to_all x0 -> x1, starting transfers between devices: none -> 3.51 us  [per_device(): third = lax.all_to_all(pair, 'ta', 0, 0, tiled=True)]
    unnamed x7 -> x13, local copies, waits for them, and re-layouts: 3.91 us -> 0.72 us
    all_to_all x0 -> x1, waiting for transfers between devices: none -> 2.2 us  [per_device(): third = lax.all_to_all(pair, 'ta', 0, 0, tiled=True)]
    pallas_call x1, Pallas kernels: 1.72 us -> 0.1 us  [per_device(): pl.pallas_call(functools.partial(pack_grads, n_af, n_sa), out_shape=[jax....]
    pallas_call x1, Pallas kernels: 1.62 us -> 0.67 us  [per_device(): pl.pallas_call(functools.partial(update, n_af, n_sa), out_shape=[jax.Shap...]
  transfers between devices with their start and end apart: 1 -> 2, of which waited for: 1 -> 2; matrix products, arithmetic and copies ran while one was open for 1% -> 1% of each run, Pallas kernels for 0% -> 7%
where the time goes in v2:
time: 78.7 us; the launch traced here: 78.2 us
  blocking collectives  39.4 us (50%)
  Pallas kernels  13.6 us (17%)
  starting transfers between devices  13.5 us (17%)
  waiting for transfers between devices  8.79 us (11%)
  between operations  1.4 us (2%)
    all_to_all x1, blocking collectives, per_device(): first = lax.all_to_all(packed, ('af', 'sa'), 0, 0, tiled=True)  21.8 us
    all_to_all x1, blocking collectives, per_device(): fourth = lax.all_to_all(packed_grads, ('af', 'sa'), 0, 0, tiled=True)  17.6 us
    all_to_all x1, starting transfers between devices, per_device(): second = lax.all_to_all(joined, 'ta', 0, 0, tiled=True)  10 us
    all_to_all x1, waiting for transfers between devices, per_device(): second = lax.all_to_all(joined, 'ta', 0, 0, tiled=True)  6.59 us
    pallas_call x1, Pallas kernels, pair_grads(): kernel_call(functools.partial(pair_body, n_freq), jax.ShapeDtypeStruct(se...  6.51 us
    pallas_call x1, Pallas kernels, time_grads(): kernel_call(functools.partial(time_body, n_freq), jax.ShapeDtypeStruct((2...  5.63 us
    all_to_all x1, starting transfers between devices, per_device(): third = lax.all_to_all(pair, 'ta', 0, 0, tiled=True)  3.51 us
    all_to_all x1, waiting for transfers between devices, per_device(): third = lax.all_to_all(pair, 'ta', 0, 0, tiled=True)  2.2 us
  transfers between devices with their start and end apart: 2, of which 2 were waited for; matrix products, arithmetic and copies ran while one was open for 1% of the time, Pallas kernels for 7%

profile of v2, /device:TPU:1, one launch (start us, length us, event | category | flops | bytes accessed | tf_op | source)
XLA Modules:
  0.0 78.2 jit_solution(10571965612475211170)
XLA Ops:
  0.6 0.7 pad_maximum_fusion.own_ref
  1.4 21.8 %all_to_all.20.got_ref = bf16[64,8,128]{2,1,0:T(8,128)(2,1)S(1)} all-to-all(bf16[64,8,128]{2,1,0:T(8,128)(2,1)S(1)} %pack_factors.1.packed_ref), channel_id=1, replica_groups=mesh['ta'=8,'af'=8,'sa'=8] {'af','sa'}, dimensions={0} | all-to-all | bytes 262144 | tf_op jit(solution)/shard_map/all_to_all | solution.py:327
  23.1 0.7 join_factors.1
  23.8 10.0 %all-to-all-start.1 = ((bf16[8,32,256]{2,1,0:T(8,128)(2,1)}), bf16[8,32,256]{2,1,0:T(8,128)(2,1)S(1)}, u32[]{:S(2)}, u32[]{:S(2)}) async-start(bf16[8,32,256]{2,1,0:T(8,128)(2,1)} %get-tuple-element.11), calls=%async_computation.1 | async-start | bytes 262144 | tf_op jit(solution)/shard_map/all_to_all | solution.py:342
  33.9 0.7 copy.17
  35.2 6.6 %all-to-all-done.1.second_ref = bf16[8,32,256]{2,1,0:T(8,128)(2,1)S(1)} async-done(((bf16[8,32,256]{2,1,0:T(8,128)(2,1)}), bf16[8,32,256]{2,1,0:T(8,128)(2,1)S(1)}, u32[]{:S(2)}, u32[]{:S(2)}) %all-to-all-start.1) | async-done | bytes 131104 | tf_op jit(solution)/shard_map/all_to_all | solution.py:342
  41.8 6.5 %pair_grads.1 = bf16[8,32,256]{2,1,0:T(8,128)(2,1)} custom-call(s32[4,4]{1,0:T(4,128)S(1)} %concatenate.6.where_ref, bf16[1,1,1,4,64,4096]{5,4,3,2,1,0:T(8,128)(2,1)} %blocks_ref.3, bf16[128,256]{1,0:T(8,128)(2,1)S(1)} %get-tuple-element.10.time_ref, bf16[8,32,256]{2,1,0:T(8,128)(2,1)S(1)} %all-to-all-done.1.second_ref), custom_call_target="tpu_custom_call" | custom-call | flops 536870912 | bytes 2684354 | tf_op jit(solution)/shard_map/pair_grads/pallas_call | solution.py:206
  48.3 0.0 copy-start
  48.4 0.0 copy-start.1
  48.4 0.0 copy-start.2
  48.4 0.0 copy-start.3
  48.4 0.0 copy-start.4
  48.4 0.0 copy-start.5
  48.4 3.5 %all-to-all-start.2 = ((bf16[8,32,256]{2,1,0:T(8,128)(2,1)}), bf16[8,32,256]{2,1,0:T(8,128)(2,1)S(1)}, u32[]{:S(2)}, u32[]{:S(2)}) async-start(bf16[8,32,256]{2,1,0:T(8,128)(2,1)} %pair_grads.1), calls=%async_computation.2 | async-start | bytes 262144 | tf_op jit(solution)/shard_map/all_to_all | solution.py:345
  51.9 5.6 %time_grads.1.time_ref = f32[2,128,128]{2,1,0:T(8,128)S(1)} custom-call(s32[4,4]{1,0:T(4,128)S(1)} %concatenate.6.where_ref, bf16[1,1,1,4,64,4096]{5,4,3,2,1,0:T(8,128)(2,1)} %blocks_ref.3, bf16[128,256]{1,0:T(8,128)(2,1)S(1)} %get-tuple-element.10.time_ref, bf16[8,32,256]{2,1,0:T(8,128)(2,1)S(1)} %all-to-all-done.1.second_ref), custom_call_target="tpu_custom_call" | custom-call | flops 536870912 | bytes 2684354 | tf_op jit(solution)/shard_map/time_grads/pallas_call | solution.py:226
  57.6 2.2 %all-to-all-done.2.got_ref = bf16[8,32,256]{2,1,0:T(8,128)(2,1)S(1)} async-done(((bf16[8,32,256]{2,1,0:T(8,128)(2,1)}), bf16[8,32,256]{2,1,0:T(8,128)(2,1)S(1)}, u32[]{:S(2)}, u32[]{:S(2)}) %all-to-all-start.2) | async-done | bytes 131104 | tf_op jit(solution)/shard_map/all_to_all | solution.py:345
  59.8 0.1 pack_grads.1
  59.9 17.6 %all_to_all.21.got_ref = bf16[64,8,128]{2,1,0:T(8,128)(2,1)S(1)} all-to-all(bf16[64,8,128]{2,1,0:T(8,128)(2,1)S(1)} %get-tuple-element.12), channel_id=1, replica_groups=mesh['ta'=8,'af'=8,'sa'=8] {'af','sa'}, dimensions={0} | all-to-all | bytes 262144 | tf_op jit(solution)/shard_map/all_to_all | solution.py:359
  77.5 0.0 copy-done
  77.5 0.0 copy-done.1
  77.5 0.0 copy-done.2
  77.5 0.0 copy-done.3
  77.5 0.0 copy-done.4
  77.5 0.0 copy-done.5
  77.5 0.7 update.1
  (2 shorter events, 0.0 us)
Async XLA Ops:
  23.8 18.0 %all-to-all-start.1 = ((bf16[8,32,256]{2,1,0:T(8,128)(2,1)}), bf16[8,32,256]{2,1,0:T(8,128)(2,1)S(1)}, u32[]{:S(2)}, u32[]{:S(2)}) async-start(bf16[8,32,256]{2,1,0:T(8,128)(2,1)} %get-tuple-element.11), calls=%async_computation.1 | async-start | bytes 262144 | tf_op jit(solution)/shard_map/all_to_all | solution.py:342
  48.3 29.1 %copy-start = (f32[1,2,256]{2,1,0:T(2,128)S(1)}, f32[1,2,256]{2,1,0:T(2,128)}, u32[]{:S(2)}) copy-start(f32[1,2,256]{2,1,0:T(2,128)} %subj_ref.1) | copy-start | bytes 6148
  48.4 29.1 %copy-start.1 = (f32[1,2,256]{2,1,0:T(2,128)S(1)}, f32[1,2,256]{2,1,0:T(2,128)}, u32[]{:S(2)}) copy-start(f32[1,2,256]{2,1,0:T(2,128)} %freq_ref.1) | copy-start | bytes 6148
  48.4 29.1 %copy-start.2 = (f32[1,2,256]{2,1,0:T(2,128)S(1)}, f32[1,2,256]{2,1,0:T(2,128)}, u32[]{:S(2)}) copy-start(f32[1,2,256]{2,1,0:T(2,128)} %time_ref.1) | copy-start | bytes 6148
  48.4 29.1 %copy-start.3 = (f32[1,2,256]{2,1,0:T(2,128)S(1)}, f32[1,2,256]{2,1,0:T(2,128)}, u32[]{:S(2)}) copy-start(f32[1,2,256]{2,1,0:T(2,128)} %time_vel_ref.1) | copy-start | bytes 6148
  48.4 29.1 %copy-start.4 = (f32[1,2,256]{2,1,0:T(2,128)S(1)}, f32[1,2,256]{2,1,0:T(2,128)}, u32[]{:S(2)}) copy-start(f32[1,2,256]{2,1,0:T(2,128)} %freq_vel_ref.1) | copy-start | bytes 6148
  48.4 29.1 %copy-start.5 = (f32[1,2,256]{2,1,0:T(2,128)S(1)}, f32[1,2,256]{2,1,0:T(2,128)}, u32[]{:S(2)}) copy-start(f32[1,2,256]{2,1,0:T(2,128)} %subj_vel_ref.1) | copy-start | bytes 6148
  48.4 11.4 %all-to-all-start.2 = ((bf16[8,32,256]{2,1,0:T(8,128)(2,1)}), bf16[8,32,256]{2,1,0:T(8,128)(2,1)S(1)}, u32[]{:S(2)}, u32[]{:S(2)}) async-start(bf16[8,32,256]{2,1,0:T(8,128)(2,1)} %pair_grads.1), calls=%async_computation.2 | async-start | bytes 262144 | tf_op jit(solution)/shard_map/all_to_all | solution.py:345

commit v3 on v2

--- a/solution.py
+++ b/solution.py
@@ -11,7 +11,8 @@
 F32 = jnp.float32
 ROWS = 2
 HALF = 128
-BIG = 56 * 1000 * 1000
+BIG = 24 << 20
+FETCH = 53 * 1000 * 1000
 SMALL = 4 << 20
 SEND = BF16
 
@@ -85,30 +86,39 @@
     return freq.reshape(-1, rank), subj.reshape(-1, rank)
 
 
-def fetch_blocks(blocks_ref, data, sems):
+def fetch_body(blocks_ref, time_ref, data_ref, grams_ref, sems):
+    cap, bt, cells = data_ref.shape
+    parts = sems.shape[1]
+    rows = bt // parts
     copies = [
-        pltpu.make_async_copy(blocks_ref.at[0, 0, 0, slot], data.at[slot], sems.at[slot])
-        for slot in range(data.shape[0])
+        pltpu.make_async_copy(
+            blocks_ref.at[0, 0, 0, slot, pl.ds(part * rows, rows)],
+            data_ref.at[slot, pl.ds(part * rows, rows)],
+            sems.at[slot, part],
+        )
+        for slot in range(cap)
+        for part in range(parts)
     ]
     for copy in copies:
         copy.start()
-    return copies
+    for which in range(2):
+        grams_ref[which] = gram(take(time_ref, which, time_ref.shape[0] // 2))
+    for copy in copies:
+        copy.wait()
 
 
 def pair_body(
     n_freq,
     where_ref,
-    blocks_ref,
+    data_ref,
     time_ref,
+    time_grams_ref,
     second_ref,
     pair_ref,
-    data,
     grams,
     freq,
     subj,
-    sems,
 ):
-    copies = fetch_blocks(blocks_ref, data, sems)
     n_ta = second_ref.shape[0]
     bf = freq.shape[0] // 2
     bs = subj.shape[0] // 2
@@ -118,70 +128,54 @@
     subj[...] = jnp.zeros_like(subj)
     for which in range(2):
         b, c = pair_blocks(second_ref, which, which, n_freq)
-        grams[which] = gram(take(time_ref, which, bt))
-        grams[2 + which] = gram(b)
-        grams[4 + which] = gram(c)
+        grams[which] = gram(b)
+        grams[2 + which] = gram(c)
     step = min(8, bf)
-    for slot, copy in enumerate(copies):
-        copy.wait()
-
-        @pl.when(slot < where_ref[3, slot])
-        def _(slot=slot):
-            time_at = where_ref[0, slot]
-            freq_at = where_ref[1, slot]
-            subj_at = where_ref[2, slot]
-            a = take(time_ref, time_at, bt)
-            b, c = pair_blocks(second_ref, freq_at, subj_at, n_freq)
-            time_gram = grams[time_at]
-            freq_model = model_part(b, time_gram * grams[4 + subj_at])
-            subj_model = model_part(c, time_gram * grams[2 + freq_at])
-            wide_b, wide_c = b.astype(F32), c.astype(F32)
-            freq_data = []
-            subj_data = jnp.zeros(wide_c.shape, F32)
-            for j in range(0, bf, step):
-                cells = data[slot, :, j * bs : (j + step) * bs]
-                cube = dot(cells, a, ((0,), (0,))).reshape(step, bs, -1)
-                freq_data.append(jnp.sum(cube * wide_c[None], axis=1))
-                for k in range(step):
-                    subj_data += cube[k] * wide_b[j + k : j + k + 1]
-            freq_data = jnp.concatenate(freq_data, axis=0)
-            freq[pl.ds(pl.multiple_of(freq_at * bf, bf), bf), :] += freq_model - freq_data
-            subj[pl.ds(pl.multiple_of(subj_at * bs, bs), bs), :] += subj_model - subj_data
+    for slot in range(data_ref.shape[0]):
+        live = slot < where_ref[3, slot]
+        time_at = where_ref[0, slot]
+        freq_at = where_ref[1, slot]
+        subj_at = where_ref[2, slot]
+        a = take(time_ref, time_at, bt)
+        b, c = pair_blocks(second_ref, freq_at, subj_at, n_freq)
+        time_gram = time_grams_ref[time_at]
+        freq_model = model_part(b, time_gram * grams[2 + subj_at])
+        subj_model = model_part(c, time_gram * grams[freq_at])
+        wide_b, wide_c = b.astype(F32), c.astype(F32)
+        freq_data = []
+        subj_data = jnp.zeros(wide_c.shape, F32)
+        for j in range(0, bf, step):
+            cells = data_ref[slot, :, j * bs : (j + step) * bs]
+            cube = dot(cells, a, ((0,), (0,))).reshape(step, bs, -1)
+            freq_data.append(jnp.sum(cube * wide_c[None], axis=1))
+            for k in range(step):
+                subj_data += cube[k] * wide_b[j + k : j + k + 1]
+        freq_data = jnp.concatenate(freq_data, axis=0)
+        freq_grad = jnp.where(live, freq_model - freq_data, 0.0)
+        subj_grad = jnp.where(live, subj_model - subj_data, 0.0)
+        freq[pl.ds(pl.multiple_of(freq_at * bf, bf), bf), :] += freq_grad
+        subj[pl.ds(pl.multiple_of(subj_at * bs, bs), bs), :] += subj_grad
 
     for t in range(n_ta):
         pair_ref[t, :n_freq, :] = freq[t * n_freq : (t + 1) * n_freq, :].astype(SEND)
         pair_ref[t, n_freq:, :] = subj[t * n_subj : (t + 1) * n_subj, :].astype(SEND)
 
 
-def time_body(
-    n_freq, where_ref, blocks_ref, time_ref, second_ref, out_ref, data, grad, sems
-):
-    copies = fetch_blocks(blocks_ref, data, sems)
-    bt = data.shape[1]
+def time_body(n_freq, where_ref, data_ref, time_ref, second_ref, out_ref, grad):
+    bt = data_ref.shape[1]
     grad[...] = jnp.zeros_like(grad)
-    for slot, copy in enumerate(copies):
-        copy.wait()
-
-        @pl.when(slot < where_ref[3, slot])
-        def _(slot=slot):
-            time_at = where_ref[0, slot]
-            a = take(time_ref, time_at, bt)
-            b, c = pair_blocks(
-                second_ref, where_ref[1, slot], where_ref[2, slot], n_freq
-            )
-            bf, bs = b.shape[0], c.shape[0]
-            total = model_part(a, gram(b) * gram(c))
-            wide_b = b.astype(F32)
-            zero = jnp.zeros_like(c)
-            both = jnp.concatenate(
-                [jnp.concatenate([c, zero], axis=1), jnp.concatenate([zero, c], axis=1)], axis=0
-            )
-            rank = c.shape[1]
-            for j in range(0, bf, 2):
-                part = dot(data[slot, :, j * bs : (j + 2) * bs], both)
-                total -= part[:, :rank] * wide_b[j : j + 1]
-                total -= part[:, rank:] * wide_b[j + 1 : j + 2]
-            grad[pl.ds(pl.multiple_of(time_at * bt, bt), bt), :] += total
+    for slot in range(data_ref.shape[0]):
+        live = slot < where_ref[3, slot]
+        time_at = where_ref[0, slot]
+        a = take(time_ref, time_at, bt)
+        b, c = pair_blocks(second_ref, where_ref[1, slot], where_ref[2, slot], n_freq)
+        bf, bs = b.shape[0], c.shape[0]
+        step = min(8, bf)
+        total = model_part(a, gram(b) * gram(c))
+        for j in range(0, bf, step):
+            khatri = (b[j : j + step][:, None, :] * c[None]).reshape(step * bs, -1)
+            total -= dot(data_ref[slot, :, j * bs : (j + step) * bs], khatri)
+        grad[pl.ds(pl.multiple_of(time_at * bt, bt), bt), :] += jnp.where(live, total, 0.0)
 
     for half in range(2):
         out_ref[half] = grad[:, half * HALF : (half + 1) * HALF]
@@ -200,42 +194,50 @@
     )
 
 
-def pair_grads(n_freq, n_subj, slots_of, blocks, time_table, second):
+def fetch(blocks, time_table):
     cap, bt, cells = blocks.shape[3:]
+    rank = time_table.shape[1]
+    return kernel_call(
+        fetch_body,
+        [
+            jax.ShapeDtypeStruct((cap, bt, cells), BF16),
+            jax.ShapeDtypeStruct((2, rank, rank), F32),
+        ],
+        [pltpu.HBM, pltpu.VMEM],
+        [pltpu.SemaphoreType.DMA((cap, 4))],
+        "fetch",
+        cap * bt * cells * 4,
+        FETCH,
+    )(blocks, time_table)
+
+
+def pair_grads(n_freq, n_subj, slots_of, data, time_table, time_grams, second):
     n_ta, rows, rank = second.shape
     return kernel_call(
         functools.partial(pair_body, n_freq),
         jax.ShapeDtypeStruct(second.shape, SEND),
-        [pltpu.SMEM, pltpu.HBM, pltpu.VMEM, pltpu.VMEM],
+        [pltpu.SMEM] + [pltpu.VMEM] * 4,
         [
-            pltpu.VMEM((cap, bt, cells), BF16),
-            pltpu.VMEM((6, rank, rank), F32),
+            pltpu.VMEM((4, rank, rank), F32),
             pltpu.VMEM((n_ta * n_freq, rank), F32),
             pltpu.VMEM((n_ta * n_subj, rank), F32),
-            pltpu.SemaphoreType.DMA((cap,)),
         ],
         "pair_grads",
-        2 * cap * bt * cells * rank,
+        2 * data.size * rank,
         BIG,
-    )(slots_of, blocks, time_table, second)
-
-
-def time_grads(n_freq, slots_of, blocks, time_table, second):
-    cap, bt, cells = blocks.shape[3:]
-    rank = time_table.shape[1]
+    )(slots_of, data, time_table, time_grams, second)
+
+
+def time_grads(n_freq, slots_of, data, time_table, second):
     return kernel_call(
         functools.partial(time_body, n_freq),
         jax.ShapeDtypeStruct((2, time_table.shape[0], HALF), F32),
-        [pltpu.SMEM, pltpu.HBM, pltpu.VMEM, pltpu.VMEM],
-        [
-            pltpu.VMEM((cap, bt, cells), BF16),
-            pltpu.VMEM(time_table.shape, F32),
-            pltpu.SemaphoreType.DMA((cap,)),
-        ],
+        [pltpu.SMEM] + [pltpu.VMEM] * 3,
+        [pltpu.VMEM(time_table.shape, F32)],
         "time_grads",
-        2 * cap * bt * cells * rank,
+        2 * data.size * time_table.shape[1],
         BIG,
-    )(slots_of, blocks, time_table, second)
+    )(slots_of, data, time_table, second)
 
 
 def pack_grads(n_af, n_sa, got_ref, time_ref, out_ref, own_ref, summed, wide):
@@ -340,8 +342,10 @@
         name="join_factors",
     )(first, packed)
     second = lax.all_to_all(joined, "ta", 0, 0, tiled=True)
-    pair = pair_grads(ROWS * n_sa, ROWS * n_af, slots_of, blocks, time_table, second)
-    time_grad = time_grads(ROWS * n_sa, slots_of, blocks, time_table, second)
+    data, time_grams = fetch(blocks, time_table)
+    n_freq, n_subj = ROWS * n_sa, ROWS * n_af
+    pair = pair_grads(n_freq, n_subj, slots_of, data, time_table, time_grams, second)
+    time_grad = time_grads(n_freq, slots_of, data, time_table, second)
     third = lax.all_to_all(pair, "ta", 0, 0, tiled=True)
     packed_grads, own = pl.pallas_call(
         functools.partial(pack_grads, n_af, n_sa),

time: 78.7 us -> 77.5 us (0.985)
  Pallas kernels: 13.6 us -> 11.6 us
  waiting for transfers between devices: 8.79 us -> 9.65 us
    pallas_call x1, Pallas kernels: 5.63 us -> 3.02 us  [time_grads(): kernel_call(functools.partial(time_body, n_freq), jax.ShapeDtypeStruct((2...]
    all_to_all x1, waiting for transfers between devices: 2.2 us -> 4.81 us  [per_device(): third = lax.all_to_all(pair, 'ta', 0, 0, tiled=True)]
    all_to_all x1, waiting for transfers between devices: 6.59 us -> 4.84 us  [per_device(): second = lax.all_to_all(joined, 'ta', 0, 0, tiled=True)]
    pallas_call x0 -> x1, Pallas kernels: none -> 1.74 us  [fetch(): kernel_call(fetch_body, [jax.ShapeDtypeStruct((cap, bt, cells), BF16), ja...]
    pallas_call x1, Pallas kernels: 6.51 us -> 5.33 us  [pair_grads(): kernel_call(functools.partial(pair_body, n_freq), jax.ShapeDtypeStruct(se...]
  transfers between devices with their start and end apart: 2 -> 2, of which waited for: 2 -> 2; matrix products, arithmetic and copies ran while one was open for 1% -> 1% of each run, Pallas kernels for 7% -> 6%
where the time goes in v3:
time: 77.5 us; the launch traced here: 77 us
  blocking collectives  39.4 us (51%)
  starting transfers between devices  13.5 us (17%)
  Pallas kernels  11.6 us (15%)
  waiting for transfers between devices  9.65 us (12%)
  between operations  1.37 us (2%)
    all_to_all x1, blocking collectives, per_device(): first = lax.all_to_all(packed, ('af', 'sa'), 0, 0, tiled=True)  21.8 us
    all_to_all x1, blocking collectives, per_device(): fourth = lax.all_to_all(packed_grads, ('af', 'sa'), 0, 0, tiled=True)  17.7 us
    all_to_all x1, starting transfers between devices, per_device(): second = lax.all_to_all(joined, 'ta', 0, 0, tiled=True)  10 us
    pallas_call x1, Pallas kernels, pair_grads(): kernel_call(functools.partial(pair_body, n_freq), jax.ShapeDtypeStruct(se...  5.33 us
    all_to_all x1, waiting for transfers between devices, per_device(): second = lax.all_to_all(joined, 'ta', 0, 0, tiled=True)  4.84 us
    all_to_all x1, waiting for transfers between devices, per_device(): third = lax.all_to_all(pair, 'ta', 0, 0, tiled=True)  4.81 us
    all_to_all x1, starting transfers between devices, per_device(): third = lax.all_to_all(pair, 'ta', 0, 0, tiled=True)  3.51 us
    pallas_call x1, Pallas kernels, time_grads(): kernel_call(functools.partial(time_body, n_freq), jax.ShapeDtypeStruct((2...  3.02 us
  transfers between devices with their start and end apart: 2, of which 2 were waited for; matrix products, arithmetic and copies ran while one was open for 1% of the time, Pallas kernels for 6%

profile of v3, /device:TPU:1, one launch (start us, length us, event | category | flops | bytes accessed | tf_op | source)
XLA Modules:
  0.0 77.0 jit_solution(8447461810625992151)
XLA Ops:
  0.6 0.7 pad_maximum_fusion.own_ref
  1.4 21.8 %all_to_all.20.got_ref = bf16[64,8,128]{2,1,0:T(8,128)(2,1)S(1)} all-to-all(bf16[64,8,128]{2,1,0:T(8,128)(2,1)S(1)} %pack_factors.1.packed_ref), channel_id=1, replica_groups=mesh['ta'=8,'af'=8,'sa'=8] {'af','sa'}, dimensions={0} | all-to-all | bytes 262144 | tf_op jit(solution)/shard_map/all_to_all | solution.py:329
  23.1 0.7 join_factors.1
  23.9 10.0 %all-to-all-start.1 = ((bf16[8,32,256]{2,1,0:T(8,128)(2,1)}), bf16[8,32,256]{2,1,0:T(8,128)(2,1)S(1)}, u32[]{:S(2)}, u32[]{:S(2)}) async-start(bf16[8,32,256]{2,1,0:T(8,128)(2,1)} %get-tuple-element.15), calls=%async_computation.1 | async-start | bytes 262144 | tf_op jit(solution)/shard_map/all_to_all | solution.py:344
  34.5 0.7 copy.17
  35.2 1.7 %fetch.1 = (bf16[4,64,4096]{2,1,0:T(8,128)(2,1)S(1)}, f32[2,256,256]{2,1,0:T(8,128)S(1)}) custom-call(bf16[1,1,1,4,64,4096]{5,4,3,2,1,0:T(8,128)(2,1)} %blocks_ref.1, bf16[128,256]{1,0:T(8,128)(2,1)S(1)} %get-tuple-element.12.time_ref), custom_call_target="tpu_custom_call" | custom-call | flops 4194304 | bytes 20971 | tf_op jit(solution)/shard_map/fetch/pallas_call | solution.py:200
  37.0 4.8 %all-to-all-done.1.second_ref = bf16[8,32,256]{2,1,0:T(8,128)(2,1)S(1)} async-done(((bf16[8,32,256]{2,1,0:T(8,128)(2,1)}), bf16[8,32,256]{2,1,0:T(8,128)(2,1)S(1)}, u32[]{:S(2)}, u32[]{:S(2)}) %all-to-all-start.1) | async-done | bytes 131104 | tf_op jit(solution)/shard_map/all_to_all | solution.py:344
  41.8 5.3 %pair_grads.1 = bf16[8,32,256]{2,1,0:T(8,128)(2,1)} custom-call(s32[4,4]{1,0:T(4,128)S(1)} %concatenate.6.where_ref, bf16[4,64,4096]{2,1,0:T(8,128)(2,1)S(1)} %get-tuple-element.13.data_ref, bf16[128,256]{1,0:T(8,128)(2,1)S(1)} %get-tuple-element.12.time_ref, f32[2,256,256]{2,1,0:T(8,128)S(1)} %get-tuple-element.14.time_grams_ref, ...), custom_call_target="tpu_custom_call" | custom-call | flops 536870912 | bytes 2684354 | tf_op jit(solution)/shard_map/pair_grads/pallas_call | solution.py:216
  47.2 0.0 copy-start
  47.2 0.0 copy-start.1
  47.2 0.0 copy-start.2
  47.2 0.0 copy-start.3
  47.2 0.0 copy-start.4
  47.2 0.0 copy-start.5
  47.2 3.5 %all-to-all-start.2 = ((bf16[8,32,256]{2,1,0:T(8,128)(2,1)}), bf16[8,32,256]{2,1,0:T(8,128)(2,1)S(1)}, u32[]{:S(2)}, u32[]{:S(2)}) async-start(bf16[8,32,256]{2,1,0:T(8,128)(2,1)} %pair_grads.1), calls=%async_computation.2 | async-start | bytes 262144 | tf_op jit(solution)/shard_map/all_to_all | solution.py:349
  50.7 3.0 %time_grads.1.time_ref = f32[2,128,128]{2,1,0:T(8,128)S(1)} custom-call(s32[4,4]{1,0:T(4,128)S(1)} %concatenate.6.where_ref, bf16[4,64,4096]{2,1,0:T(8,128)(2,1)S(1)} %get-tuple-element.13.data_ref, bf16[128,256]{1,0:T(8,128)(2,1)S(1)} %get-tuple-element.12.time_ref, bf16[8,32,256]{2,1,0:T(8,128)(2,1)S(1)} %all-to-all-done.1.second_ref), custom_call_target="tpu_custom_call" | custom-call | flops 536870912 | bytes 2684354 | tf_op jit(solution)/shard_map/time_grads/pallas_call | solution.py:232
  53.7 4.8 %all-to-all-done.2.got_ref = bf16[8,32,256]{2,1,0:T(8,128)(2,1)S(1)} async-done(((bf16[8,32,256]{2,1,0:T(8,128)(2,1)}), bf16[8,32,256]{2,1,0:T(8,128)(2,1)S(1)}, u32[]{:S(2)}, u32[]{:S(2)}) %all-to-all-start.2) | async-done | bytes 131104 | tf_op jit(solution)/shard_map/all_to_all | solution.py:349
  58.6 0.1 pack_grads.1
  58.7 17.7 %all_to_all.21.got_ref = bf16[64,8,128]{2,1,0:T(8,128)(2,1)S(1)} all-to-all(bf16[64,8,128]{2,1,0:T(8,128)(2,1)S(1)} %get-tuple-element.16), channel_id=1, replica_groups=mesh['ta'=8,'af'=8,'sa'=8] {'af','sa'}, dimensions={0} | all-to-all | bytes 262144 | tf_op jit(solution)/shard_map/all_to_all | solution.py:363
  76.3 0.0 copy-done
  76.3 0.0 copy-done.1
  76.3 0.0 copy-done.2
  76.3 0.0 copy-done.3
  76.3 0.0 copy-done.4
  76.3 0.0 copy-done.5
  76.4 0.7 update.1
  (2 shorter events, 0.0 us)
Async XLA Ops:
  23.9 18.0 %all-to-all-start.1 = ((bf16[8,32,256]{2,1,0:T(8,128)(2,1)}), bf16[8,32,256]{2,1,0:T(8,128)(2,1)S(1)}, u32[]{:S(2)}, u32[]{:S(2)}) async-start(bf16[8,32,256]{2,1,0:T(8,128)(2,1)} %get-tuple-element.15), calls=%async_computation.1 | async-start | bytes 262144 | tf_op jit(solution)/shard_map/all_to_all | solution.py:344
  47.2 29.1 %copy-start = (f32[1,2,256]{2,1,0:T(2,128)S(1)}, f32[1,2,256]{2,1,0:T(2,128)}, u32[]{:S(2)}) copy-start(f32[1,2,256]{2,1,0:T(2,128)} %subj_ref.1) | copy-start | bytes 6148
  47.2 29.2 %copy-start.1 = (f32[1,2,256]{2,1,0:T(2,128)S(1)}, f32[1,2,256]{2,1,0:T(2,128)}, u32[]{:S(2)}) copy-start(f32[1,2,256]{2,1,0:T(2,128)} %freq_ref.1) | copy-start | bytes 6148
  47.2 29.2 %copy-start.2 = (f32[1,2,256]{2,1,0:T(2,128)S(1)}, f32[1,2,256]{2,1,0:T(2,128)}, u32[]{:S(2)}) copy-start(f32[1,2,256]{2,1,0:T(2,128)} %time_ref.1) | copy-start | bytes 6148
  47.2 29.2 %copy-start.3 = (f32[1,2,256]{2,1,0:T(2,128)S(1)}, f32[1,2,256]{2,1,0:T(2,128)}, u32[]{:S(2)}) copy-start(f32[1,2,256]{2,1,0:T(2,128)} %time_vel_ref.1) | copy-start | bytes 6148
  47.2 29.2 %copy-start.4 = (f32[1,2,256]{2,1,0:T(2,128)S(1)}, f32[1,2,256]{2,1,0:T(2,128)}, u32[]{:S(2)}) copy-start(f32[1,2,256]{2,1,0:T(2,128)} %freq_vel_ref.1) | copy-start | bytes 6148
  47.2 29.2 %copy-start.5 = (f32[1,2,256]{2,1,0:T(2,128)S(1)}, f32[1,2,256]{2,1,0:T(2,128)}, u32[]{:S(2)}) copy-start(f32[1,2,256]{2,1,0:T(2,128)} %subj_vel_ref.1) | copy-start | bytes 6148
  47.2 11.4 %all-to-all-start.2 = ((bf16[8,32,256]{2,1,0:T(8,128)(2,1)}), bf16[8,32,256]{2,1,0:T(8,128)(2,1)S(1)}, u32[]{:S(2)}, u32[]{:S(2)}) async-start(bf16[8,32,256]{2,1,0:T(8,128)(2,1)} %pair_grads.1), calls=%async_computation.2 | async-start | bytes 262144 | tf_op jit(solution)/shard_map/all_to_all | solution.py:349

commit v4 on v3

--- a/solution.py
+++ b/solution.py
@@ -34,7 +34,7 @@
     out_ref[pl.ds(mine * n_sa, n_sa)] = jnp.broadcast_to(freq_tile[None], (n_sa, 8, HALF))
 
 
-def join_factors(n_af, n_sa, got_ref, packed_ref, out_ref, time_ref, wide, joined, time_table):
+def join_factors(n_af, n_sa, got_ref, packed_ref, out_ref, wide, joined):
     af = lax.axis_index("af")
     sa = lax.axis_index("sa")
     slots = n_af * n_sa
@@ -52,12 +52,6 @@
     rows = jnp.concatenate([joined[0], joined[1]], axis=1).astype(BF16)
     for peer in range(out_ref.shape[0]):
         out_ref[peer] = rows
-    for half in range(2):
-        for row in range(ROWS):
-            time_table[half, pl.ds(row, slots, stride=ROWS), :] = wide[
-                pl.ds(2 * half + row, slots, stride=8), :
-            ]
-    time_ref[...] = jnp.concatenate([time_table[0], time_table[1]], axis=1).astype(BF16)
 
 
 def dot(a, b, contract=((1,), (0,))):
@@ -86,7 +80,7 @@
     return freq.reshape(-1, rank), subj.reshape(-1, rank)
 
 
-def fetch_body(blocks_ref, time_ref, data_ref, grams_ref, sems):
+def fetch_body(blocks_ref, got_ref, data_ref, grams_ref, time_ref, sems, wide, time_table):
     cap, bt, cells = data_ref.shape
     parts = sems.shape[1]
     rows = bt // parts
@@ -101,6 +95,14 @@
     ]
     for copy in copies:
         copy.start()
+    slots = got_ref.shape[0]
+    wide[...] = got_ref[...].astype(F32).reshape(slots * 8, HALF)
+    for half in range(2):
+        for row in range(ROWS):
+            time_table[half, pl.ds(row, slots, stride=ROWS), :] = wide[
+                pl.ds(2 * half + row, slots, stride=8), :
+            ]
+    time_ref[...] = jnp.concatenate([time_table[0], time_table[1]], axis=1).astype(BF16)
     for which in range(2):
         grams_ref[which] = gram(take(time_ref, which, time_ref.shape[0] // 2))
     for copy in copies:
@@ -131,30 +133,40 @@
         grams[which] = gram(b)
         grams[2 + which] = gram(c)
     step = min(8, bf)
-    for slot in range(data_ref.shape[0]):
-        live = slot < where_ref[3, slot]
-        time_at = where_ref[0, slot]
-        freq_at = where_ref[1, slot]
-        subj_at = where_ref[2, slot]
-        a = take(time_ref, time_at, bt)
-        b, c = pair_blocks(second_ref, freq_at, subj_at, n_freq)
-        time_gram = time_grams_ref[time_at]
-        freq_model = model_part(b, time_gram * grams[2 + subj_at])
-        subj_model = model_part(c, time_gram * grams[freq_at])
-        wide_b, wide_c = b.astype(F32), c.astype(F32)
-        freq_data = []
-        subj_data = jnp.zeros(wide_c.shape, F32)
-        for j in range(0, bf, step):
-            cells = data_ref[slot, :, j * bs : (j + step) * bs]
-            cube = dot(cells, a, ((0,), (0,))).reshape(step, bs, -1)
-            freq_data.append(jnp.sum(cube * wide_c[None], axis=1))
-            for k in range(step):
-                subj_data += cube[k] * wide_b[j + k : j + k + 1]
-        freq_data = jnp.concatenate(freq_data, axis=0)
-        freq_grad = jnp.where(live, freq_model - freq_data, 0.0)
-        subj_grad = jnp.where(live, subj_model - subj_data, 0.0)
-        freq[pl.ds(pl.multiple_of(freq_at * bf, bf), bf), :] += freq_grad
-        subj[pl.ds(pl.multiple_of(subj_at * bs, bs), bs), :] += subj_grad
+    cap = data_ref.shape[0]
+    tables = []
+    for slot in range(cap):
+        a = take(time_ref, where_ref[0, slot], bt)
+        tables.append((a, *pair_blocks(second_ref, where_ref[1, slot], where_ref[2, slot], n_freq)))
+
+    def product(slot, j):
+        cells = data_ref[slot, :, j * bs : (j + step) * bs]
+        return dot(cells, tables[slot][0], ((0,), (0,))).reshape(step, bs, -1)
+
+    chunks = [(slot, j) for slot in range(cap) for j in range(0, bf, step)]
+    ahead = product(*chunks[0])
+    for at, (slot, j) in enumerate(chunks):
+        cube = ahead
+        if at + 1 < len(chunks):
+            ahead = product(*chunks[at + 1])
+        a, b, c = tables[slot]
+        if j == 0:
+            wide_b, wide_c = b.astype(F32), c.astype(F32)
+            freq_data = []
+            subj_data = jnp.zeros(wide_c.shape, F32)
+        freq_data.append(jnp.sum(cube * wide_c[None], axis=1))
+        for k in range(step):
+            subj_data += cube[k] * wide_b[j + k : j + k + 1]
+        if j + step == bf:
+            live = slot < where_ref[3, slot]
+            freq_at, subj_at = where_ref[1, slot], where_ref[2, slot]
+            time_gram = time_grams_ref[where_ref[0, slot]]
+            freq_grad = model_part(b, time_gram * grams[2 + subj_at])
+            subj_grad = model_part(c, time_gram * grams[freq_at])
+            freq_grad = jnp.where(live, freq_grad - jnp.concatenate(freq_data, axis=0), 0.0)
+            subj_grad = jnp.where(live, subj_grad - subj_data, 0.0)
+            freq[pl.ds(pl.multiple_of(freq_at * bf, bf), bf), :] += freq_grad
+            subj[pl.ds(pl.multiple_of(subj_at * bs, bs), bs), :] += subj_grad
 
     for t in range(n_ta):
         pair_ref[t, :n_freq, :] = freq[t * n_freq : (t + 1) * n_freq, :].astype(SEND)
@@ -194,21 +206,27 @@
     )
 
 
-def fetch(blocks, time_table):
+def fetch(blocks, first):
     cap, bt, cells = blocks.shape[3:]
-    rank = time_table.shape[1]
+    slots = first.shape[0]
+    table, rank = ROWS * slots, 2 * HALF
     return kernel_call(
         fetch_body,
         [
             jax.ShapeDtypeStruct((cap, bt, cells), BF16),
             jax.ShapeDtypeStruct((2, rank, rank), F32),
+            jax.ShapeDtypeStruct((table, rank), BF16),
         ],
         [pltpu.HBM, pltpu.VMEM],
-        [pltpu.SemaphoreType.DMA((cap, 4))],
+        [
+            pltpu.SemaphoreType.DMA((cap, 4)),
+            pltpu.VMEM((slots * 8, HALF), F32),
+            pltpu.VMEM((2, table, HALF), F32),
+        ],
         "fetch",
         cap * bt * cells * 4,
         FETCH,
-    )(blocks, time_table)
+    )(blocks, first)
 
 
 def pair_grads(n_freq, n_subj, slots_of, data, time_table, time_grams, second):
@@ -315,7 +333,6 @@
     slots = n_af * n_sa
     rank = time.shape[-1]
     pair_rows = ROWS * (n_sa + n_af)
-    table = ROWS * slots
     coords = coords.transpose(0, 1, 2, 4, 3).reshape(3, -1)
     slots_of = jnp.concatenate([coords, jnp.broadcast_to(counts.reshape(1, 1), (1, coords.shape[1]))])
 
@@ -327,22 +344,18 @@
         name="pack_factors",
     )(jnp.concatenate([time, freq, subj], axis=0))
     first = lax.all_to_all(packed, ("af", "sa"), 0, 0, tiled=True)
-    joined, time_table = pl.pallas_call(
+    joined = pl.pallas_call(
         functools.partial(join_factors, n_af, n_sa),
-        out_shape=[
-            jax.ShapeDtypeStruct((n_ta, pair_rows, rank), BF16),
-            jax.ShapeDtypeStruct((table, rank), BF16),
-        ],
+        out_shape=jax.ShapeDtypeStruct((n_ta, pair_rows, rank), BF16),
         scratch_shapes=[
             pltpu.VMEM((slots * 8, HALF), F32),
             pltpu.VMEM((2, pair_rows, HALF), F32),
-            pltpu.VMEM((2, table, HALF), F32),
         ],
         compiler_params=pltpu.CompilerParams(vmem_limit_bytes=SMALL),
         name="join_factors",
     )(first, packed)
     second = lax.all_to_all(joined, "ta", 0, 0, tiled=True)
-    data, time_grams = fetch(blocks, time_table)
+    data, time_grams, time_table = fetch(blocks, first)
     n_freq, n_subj = ROWS * n_sa, ROWS * n_af
     pair = pair_grads(n_freq, n_subj, slots_of, data, time_table, time_grams, second)
     time_grad = time_grads(n_freq, slots_of, data, time_table, second)

time: 77.5 us -> 77.2 us (level)
  no operation moved by 1% of the time
where the time goes in v4:
time: 77.2 us; the launch traced here: 76.7 us
  blocking collectives  39.4 us (51%)
  starting transfers between devices  13.5 us (17%)
  Pallas kernels  11.2 us (15%)
  waiting for transfers between devices  9.64 us (12%)
  between operations  1.37 us (2%)
    all_to_all x1, blocking collectives, per_device(): first = lax.all_to_all(packed, ('af', 'sa'), 0, 0, tiled=True)  21.8 us
    all_to_all x1, blocking collectives, per_device(): fourth = lax.all_to_all(packed_grads, ('af', 'sa'), 0, 0, tiled=True)  17.7 us
    all_to_all x1, starting transfers between devices, per_device(): second = lax.all_to_all(joined, 'ta', 0, 0, tiled=True)  10 us
    pallas_call x1, Pallas kernels, pair_grads(): kernel_call(functools.partial(pair_body, n_freq), jax.ShapeDtypeStruct(se...  4.99 us
    all_to_all x1, waiting for transfers between devices, per_device(): second = lax.all_to_all(joined, 'ta', 0, 0, tiled=True)  4.83 us
    all_to_all x1, waiting for transfers between devices, per_device(): third = lax.all_to_all(pair, 'ta', 0, 0, tiled=True)  4.81 us
    all_to_all x1, starting transfers between devices, per_device(): third = lax.all_to_all(pair, 'ta', 0, 0, tiled=True)  3.51 us
    pallas_call x1, Pallas kernels, time_grads(): kernel_call(functools.partial(time_body, n_freq), jax.ShapeDtypeStruct((2...  3.02 us
  transfers between devices with their start and end apart: 2, of which 2 were waited for; matrix products, arithmetic and copies ran while one was open for 1% of the time, Pallas kernels for 6%

profile of v4, /device:TPU:1, one launch (start us, length us, event | category | flops | bytes accessed | tf_op | source)
XLA Modules:
  0.0 76.7 jit_solution(4103621690336213694)
XLA Ops:
  0.6 0.7 pad_maximum_fusion.own_ref
  1.4 21.8 %all_to_all.20.got_ref = bf16[64,8,128]{2,1,0:T(8,128)(2,1)S(1)} all-to-all(bf16[64,8,128]{2,1,0:T(8,128)(2,1)S(1)} %pack_factors.1.packed_ref), channel_id=1, replica_groups=mesh['ta'=8,'af'=8,'sa'=8] {'af','sa'}, dimensions={0} | all-to-all | bytes 262144 | tf_op jit(solution)/shard_map/all_to_all | solution.py:346
  23.1 0.7 join_factors.1
  23.8 10.0 %all-to-all-start.1 = ((bf16[8,32,256]{2,1,0:T(8,128)(2,1)}), bf16[8,32,256]{2,1,0:T(8,128)(2,1)S(1)}, u32[]{:S(2)}, u32[]{:S(2)}) async-start(bf16[8,32,256]{2,1,0:T(8,128)(2,1)} %join_factors.1), calls=%async_computation.1 | async-start | bytes 262144 | tf_op jit(solution)/shard_map/all_to_all | solution.py:357
  34.5 0.7 copy.17
  35.2 1.7 %fetch.1 = (bf16[4,64,4096]{2,1,0:T(8,128)(2,1)S(1)}, f32[2,256,256]{2,1,0:T(8,128)S(1)}, bf16[128,256]{1,0:T(8,128)(2,1)S(1)}) custom-call(bf16[1,1,1,4,64,4096]{5,4,3,2,1,0:T(8,128)(2,1)} %blocks_ref.1, bf16[64,8,128]{2,1,0:T(8,128)(2,1)S(1)} %all_to_all.20.got_ref), custom_call_target="tpu_custom_call" | custom-call | flops 4194304 | bytes 20971 | tf_op jit(solution)/shard_map/fetch/pallas_call | solution.py:213
  37.0 4.8 %all-to-all-done.1.second_ref = bf16[8,32,256]{2,1,0:T(8,128)(2,1)S(1)} async-done(((bf16[8,32,256]{2,1,0:T(8,128)(2,1)}), bf16[8,32,256]{2,1,0:T(8,128)(2,1)S(1)}, u32[]{:S(2)}, u32[]{:S(2)}) %all-to-all-start.1) | async-done | bytes 131104 | tf_op jit(solution)/shard_map/all_to_all | solution.py:357
  41.8 5.0 %pair_grads.1 = bf16[8,32,256]{2,1,0:T(8,128)(2,1)} custom-call(s32[4,4]{1,0:T(4,128)S(1)} %concatenate.6.where_ref, bf16[4,64,4096]{2,1,0:T(8,128)(2,1)S(1)} %get-tuple-element.11.data_ref, bf16[128,256]{1,0:T(8,128)(2,1)S(1)} %get-tuple-element.12.time_ref, f32[2,256,256]{2,1,0:T(8,128)S(1)} %get-tuple-element.13.time_grams_ref, ...), custom_call_target="tpu_custom_call" | custom-call | flops 536870912 | bytes 2684354 | tf_op jit(solution)/shard_map/pair_grads/pallas_call | solution.py:234
  46.8 0.0 copy-start
  46.8 0.0 copy-start.1
  46.8 0.0 copy-start.2
  46.8 0.0 copy-start.3
  46.8 0.0 copy-start.4
  46.8 0.0 copy-start.5
  46.8 3.5 %all-to-all-start.2 = ((bf16[8,32,256]{2,1,0:T(8,128)(2,1)}), bf16[8,32,256]{2,1,0:T(8,128)(2,1)S(1)}, u32[]{:S(2)}, u32[]{:S(2)}) async-start(bf16[8,32,256]{2,1,0:T(8,128)(2,1)} %pair_grads.1), calls=%async_computation.2 | async-start | bytes 262144 | tf_op jit(solution)/shard_map/all_to_all | solution.py:362
  50.4 3.0 %time_grads.1.time_ref = f32[2,128,128]{2,1,0:T(8,128)S(1)} custom-call(s32[4,4]{1,0:T(4,128)S(1)} %concatenate.6.where_ref, bf16[4,64,4096]{2,1,0:T(8,128)(2,1)S(1)} %get-tuple-element.11.data_ref, bf16[128,256]{1,0:T(8,128)(2,1)S(1)} %get-tuple-element.12.time_ref, bf16[8,32,256]{2,1,0:T(8,128)(2,1)S(1)} %all-to-all-done.1.second_ref), custom_call_target="tpu_custom_call" | custom-call | flops 536870912 | bytes 2684354 | tf_op jit(solution)/shard_map/time_grads/pallas_call | solution.py:250
  53.4 4.8 %all-to-all-done.2.got_ref = bf16[8,32,256]{2,1,0:T(8,128)(2,1)S(1)} async-done(((bf16[8,32,256]{2,1,0:T(8,128)(2,1)}), bf16[8,32,256]{2,1,0:T(8,128)(2,1)S(1)}, u32[]{:S(2)}, u32[]{:S(2)}) %all-to-all-start.2) | async-done | bytes 131104 | tf_op jit(solution)/shard_map/all_to_all | solution.py:362
  58.2 0.1 pack_grads.1
  58.3 17.7 %all_to_all.21.got_ref = bf16[64,8,128]{2,1,0:T(8,128)(2,1)S(1)} all-to-all(bf16[64,8,128]{2,1,0:T(8,128)(2,1)S(1)} %get-tuple-element.14), channel_id=1, replica_groups=mesh['ta'=8,'af'=8,'sa'=8] {'af','sa'}, dimensions={0} | all-to-all | bytes 262144 | tf_op jit(solution)/shard_map/all_to_all | solution.py:376
  75.9 0.0 copy-done
  76.0 0.0 copy-done.1
  76.0 0.0 copy-done.2
  76.0 0.0 copy-done.3
  76.0 0.0 copy-done.4
  76.0 0.0 copy-done.5
  76.0 0.7 update.1
  (2 shorter events, 0.0 us)
Async XLA Ops:
  23.8 18.0 %all-to-all-start.1 = ((bf16[8,32,256]{2,1,0:T(8,128)(2,1)}), bf16[8,32,256]{2,1,0:T(8,128)(2,1)S(1)}, u32[]{:S(2)}, u32[]{:S(2)}) async-start(bf16[8,32,256]{2,1,0:T(8,128)(2,1)} %join_factors.1), calls=%async_computation.1 | async-start | bytes 262144 | tf_op jit(solution)/shard_map/all_to_all | solution.py:357
  46.8 29.1 %copy-start = (f32[1,2,256]{2,1,0:T(2,128)S(1)}, f32[1,2,256]{2,1,0:T(2,128)}, u32[]{:S(2)}) copy-start(f32[1,2,256]{2,1,0:T(2,128)} %subj_ref.1) | copy-start | bytes 6148
  46.8 29.2 %copy-start.1 = (f32[1,2,256]{2,1,0:T(2,128)S(1)}, f32[1,2,256]{2,1,0:T(2,128)}, u32[]{:S(2)}) copy-start(f32[1,2,256]{2,1,0:T(2,128)} %freq_ref.1) | copy-start | bytes 6148
  46.8 29.2 %copy-start.2 = (f32[1,2,256]{2,1,0:T(2,128)S(1)}, f32[1,2,256]{2,1,0:T(2,128)}, u32[]{:S(2)}) copy-start(f32[1,2,256]{2,1,0:T(2,128)} %time_ref.1) | copy-start | bytes 6148
  46.8 29.2 %copy-start.3 = (f32[1,2,256]{2,1,0:T(2,128)S(1)}, f32[1,2,256]{2,1,0:T(2,128)}, u32[]{:S(2)}) copy-start(f32[1,2,256]{2,1,0:T(2,128)} %time_vel_ref.1) | copy-start | bytes 6148
  46.8 29.2 %copy-start.4 = (f32[1,2,256]{2,1,0:T(2,128)S(1)}, f32[1,2,256]{2,1,0:T(2,128)}, u32[]{:S(2)}) copy-start(f32[1,2,256]{2,1,0:T(2,128)} %freq_vel_ref.1) | copy-start | bytes 6148
  46.8 29.2 %copy-start.5 = (f32[1,2,256]{2,1,0:T(2,128)S(1)}, f32[1,2,256]{2,1,0:T(2,128)}, u32[]{:S(2)}) copy-start(f32[1,2,256]{2,1,0:T(2,128)} %subj_vel_ref.1) | copy-start | bytes 6148
  46.8 11.4 %all-to-all-start.2 = ((bf16[8,32,256]{2,1,0:T(8,128)(2,1)}), bf16[8,32,256]{2,1,0:T(8,128)(2,1)S(1)}, u32[]{:S(2)}, u32[]{:S(2)}) async-start(bf16[8,32,256]{2,1,0:T(8,128)(2,1)} %pair_grads.1), calls=%async_computation.2 | async-start | bytes 262144 | tf_op jit(solution)/shard_map/all_to_all | solution.py:362

commit v5 on v4

--- a/solution.py
+++ b/solution.py
@@ -34,7 +34,7 @@
     out_ref[pl.ds(mine * n_sa, n_sa)] = jnp.broadcast_to(freq_tile[None], (n_sa, 8, HALF))
 
 
-def join_factors(n_af, n_sa, got_ref, packed_ref, out_ref, wide, joined):
+def join_factors(n_af, n_sa, got_ref, packed_ref, out_ref, wide, joined, rows, sems):
     af = lax.axis_index("af")
     sa = lax.axis_index("sa")
     slots = n_af * n_sa
@@ -49,9 +49,15 @@
             subj = wide[pl.ds(sa * 8 + at, n_af, stride=n_sa * 8), :]
             subj = jnp.where(is_own, own[at : at + 1], subj)
             joined[half, pl.ds(ROWS * n_sa + row, n_af, stride=ROWS), :] = subj
-    rows = jnp.concatenate([joined[0], joined[1]], axis=1).astype(BF16)
-    for peer in range(out_ref.shape[0]):
-        out_ref[peer] = rows
+    rows[...] = jnp.concatenate([joined[0], joined[1]], axis=1).astype(BF16)
+    copies = [
+        pltpu.make_async_copy(rows, out_ref.at[peer], sems.at[peer])
+        for peer in range(out_ref.shape[0])
+    ]
+    for copy in copies:
+        copy.start()
+    for copy in copies:
+        copy.wait()
 
 
 def dot(a, b, contract=((1,), (0,))):
@@ -126,25 +132,25 @@
     bs = subj.shape[0] // 2
     bt = time_ref.shape[0] // 2
     n_subj = second_ref.shape[1] - n_freq
+    step = min(8, bf)
+    cap = data_ref.shape[0]
+    tables = []
+    for slot in range(cap):
+        a = take(time_ref, where_ref[0, slot], bt)
+        tables.append((a, *pair_blocks(second_ref, where_ref[1, slot], where_ref[2, slot], n_freq)))
+
+    def product(slot, j):
+        cells = data_ref[slot, :, j * bs : (j + step) * bs]
+        return dot(cells, tables[slot][0], ((0,), (0,))).reshape(step, bs, -1)
+
+    chunks = [(slot, j) for slot in range(cap) for j in range(0, bf, step)]
+    ahead = product(*chunks[0])
     freq[...] = jnp.zeros_like(freq)
     subj[...] = jnp.zeros_like(subj)
     for which in range(2):
         b, c = pair_blocks(second_ref, which, which, n_freq)
         grams[which] = gram(b)
         grams[2 + which] = gram(c)
-    step = min(8, bf)
-    cap = data_ref.shape[0]
-    tables = []
-    for slot in range(cap):
-        a = take(time_ref, where_ref[0, slot], bt)
-        tables.append((a, *pair_blocks(second_ref, where_ref[1, slot], where_ref[2, slot], n_freq)))
-
-    def product(slot, j):
-        cells = data_ref[slot, :, j * bs : (j + step) * bs]
-        return dot(cells, tables[slot][0], ((0,), (0,))).reshape(step, bs, -1)
-
-    chunks = [(slot, j) for slot in range(cap) for j in range(0, bf, step)]
-    ahead = product(*chunks[0])
     for at, (slot, j) in enumerate(chunks):
         cube = ahead
         if at + 1 < len(chunks):
@@ -347,9 +353,13 @@
     joined = pl.pallas_call(
         functools.partial(join_factors, n_af, n_sa),
         out_shape=jax.ShapeDtypeStruct((n_ta, pair_rows, rank), BF16),
+        in_specs=[pl.BlockSpec(memory_space=pltpu.VMEM)] * 2,
+        out_specs=pl.BlockSpec(memory_space=pltpu.HBM),
         scratch_shapes=[
             pltpu.VMEM((slots * 8, HALF), F32),
             pltpu.VMEM((2, pair_rows, HALF), F32),
+            pltpu.VMEM((pair_rows, rank), BF16),
+            pltpu.SemaphoreType.DMA((n_ta,)),
         ],
         compiler_params=pltpu.CompilerParams(vmem_limit_bytes=SMALL),
         name="join_factors",

time: 77.2 us -> 77.3 us (level)
  no operation moved by 1% of the time
where the time goes in v5:
time: 77.3 us; the launch traced here: 76.7 us
  blocking collectives  39.4 us (51%)
  starting transfers between devices  13.6 us (18%)
  Pallas kernels  11.3 us (15%)
  waiting for transfers between devices  9.64 us (12%)
  between operations  1.38 us (2%)
    all_to_all x1, blocking collectives, per_device(): first = lax.all_to_all(packed, ('af', 'sa'), 0, 0, tiled=True)  21.8 us
    all_to_all x1, blocking collectives, per_device(): fourth = lax.all_to_all(packed_grads, ('af', 'sa'), 0, 0, tiled=True)  17.7 us
    all_to_all x1, starting transfers between devices, per_device(): second = lax.all_to_all(joined, 'ta', 0, 0, tiled=True)  10 us
    pallas_call x1, Pallas kernels, pair_grads(): kernel_call(functools.partial(pair_body, n_freq), jax.ShapeDtypeStruct(se...  4.99 us
    all_to_all x1, waiting for transfers between devices, per_device(): second = lax.all_to_all(joined, 'ta', 0, 0, tiled=True)  4.83 us
    all_to_all x1, waiting for transfers between devices, per_device(): third = lax.all_to_all(pair, 'ta', 0, 0, tiled=True)  4.81 us
    all_to_all x1, starting transfers between devices, per_device(): third = lax.all_to_all(pair, 'ta', 0, 0, tiled=True)  3.51 us
    pallas_call x1, Pallas kernels, time_grads(): kernel_call(functools.partial(time_body, n_freq), jax.ShapeDtypeStruct((2...  3.02 us
  transfers between devices with their start and end apart: 2, of which 2 were waited for; matrix products, arithmetic and copies ran while one was open for 1% of the time, Pallas kernels for 6%

profile of v5, /device:TPU:1, one launch (start us, length us, event | category | flops | bytes accessed | tf_op | source)
XLA Modules:
  0.0 76.7 jit_solution(9014052406111101404)
XLA Ops:
  0.6 0.7 pad_maximum_fusion.own_ref
  1.4 21.8 %all_to_all.20.got_ref = bf16[64,8,128]{2,1,0:T(8,128)(2,1)S(1)} all-to-all(bf16[64,8,128]{2,1,0:T(8,128)(2,1)S(1)} %pack_factors.1.packed_ref), channel_id=1, replica_groups=mesh['ta'=8,'af'=8,'sa'=8] {'af','sa'}, dimensions={0} | all-to-all | bytes 262144 | tf_op jit(solution)/shard_map/all_to_all | solution.py:352
  23.1 0.8 join_factors.1
  23.9 10.0 %all-to-all-start.1 = ((bf16[8,32,256]{2,1,0:T(8,128)(2,1)}), bf16[8,32,256]{2,1,0:T(8,128)(2,1)S(1)}, u32[]{:S(2)}, u32[]{:S(2)}) async-start(bf16[8,32,256]{2,1,0:T(8,128)(2,1)} %join_factors.1), calls=%async_computation.1 | async-start | bytes 262144 | tf_op jit(solution)/shard_map/all_to_all | solution.py:367
  34.6 0.7 copy.17
  35.3 1.7 %fetch.1 = (bf16[4,64,4096]{2,1,0:T(8,128)(2,1)S(1)}, f32[2,256,256]{2,1,0:T(8,128)S(1)}, bf16[128,256]{1,0:T(8,128)(2,1)S(1)}) custom-call(bf16[1,1,1,4,64,4096]{5,4,3,2,1,0:T(8,128)(2,1)} %blocks_ref.1, bf16[64,8,128]{2,1,0:T(8,128)(2,1)S(1)} %all_to_all.20.got_ref), custom_call_target="tpu_custom_call" | custom-call | flops 4194304 | bytes 20971 | tf_op jit(solution)/shard_map/fetch/pallas_call | solution.py:219
  37.1 4.8 %all-to-all-done.1.second_ref = bf16[8,32,256]{2,1,0:T(8,128)(2,1)S(1)} async-done(((bf16[8,32,256]{2,1,0:T(8,128)(2,1)}), bf16[8,32,256]{2,1,0:T(8,128)(2,1)S(1)}, u32[]{:S(2)}, u32[]{:S(2)}) %all-to-all-start.1) | async-done | bytes 131104 | tf_op jit(solution)/shard_map/all_to_all | solution.py:367
  41.9 5.0 %pair_grads.1 = bf16[8,32,256]{2,1,0:T(8,128)(2,1)} custom-call(s32[4,4]{1,0:T(4,128)S(1)} %concatenate.6.where_ref, bf16[4,64,4096]{2,1,0:T(8,128)(2,1)S(1)} %get-tuple-element.11.data_ref, bf16[128,256]{1,0:T(8,128)(2,1)S(1)} %get-tuple-element.12.time_ref, f32[2,256,256]{2,1,0:T(8,128)S(1)} %get-tuple-element.13.time_grams_ref, ...), custom_call_target="tpu_custom_call" | custom-call | flops 536870912 | bytes 2684354 | tf_op jit(solution)/shard_map/pair_grads/pallas_call | solution.py:240
  46.9 0.0 copy-start
  46.9 0.0 copy-start.1
  46.9 0.0 copy-start.2
  46.9 0.0 copy-start.3
  46.9 0.0 copy-start.4
  46.9 0.0 copy-start.5
  46.9 3.5 %all-to-all-start.2 = ((bf16[8,32,256]{2,1,0:T(8,128)(2,1)}), bf16[8,32,256]{2,1,0:T(8,128)(2,1)S(1)}, u32[]{:S(2)}, u32[]{:S(2)}) async-start(bf16[8,32,256]{2,1,0:T(8,128)(2,1)} %pair_grads.1), calls=%async_computation.2 | async-start | bytes 262144 | tf_op jit(solution)/shard_map/all_to_all | solution.py:372
  50.4 3.0 %time_grads.1.time_ref = f32[2,128,128]{2,1,0:T(8,128)S(1)} custom-call(s32[4,4]{1,0:T(4,128)S(1)} %concatenate.6.where_ref, bf16[4,64,4096]{2,1,0:T(8,128)(2,1)S(1)} %get-tuple-element.11.data_ref, bf16[128,256]{1,0:T(8,128)(2,1)S(1)} %get-tuple-element.12.time_ref, bf16[8,32,256]{2,1,0:T(8,128)(2,1)S(1)} %all-to-all-done.1.second_ref), custom_call_target="tpu_custom_call" | custom-call | flops 536870912 | bytes 2684354 | tf_op jit(solution)/shard_map/time_grads/pallas_call | solution.py:256
  53.5 4.8 %all-to-all-done.2.got_ref = bf16[8,32,256]{2,1,0:T(8,128)(2,1)S(1)} async-done(((bf16[8,32,256]{2,1,0:T(8,128)(2,1)}), bf16[8,32,256]{2,1,0:T(8,128)(2,1)S(1)}, u32[]{:S(2)}, u32[]{:S(2)}) %all-to-all-start.2) | async-done | bytes 131104 | tf_op jit(solution)/shard_map/all_to_all | solution.py:372
  58.3 0.1 pack_grads.1
  58.4 17.7 %all_to_all.21.got_ref = bf16[64,8,128]{2,1,0:T(8,128)(2,1)S(1)} all-to-all(bf16[64,8,128]{2,1,0:T(8,128)(2,1)S(1)} %get-tuple-element.14), channel_id=1, replica_groups=mesh['ta'=8,'af'=8,'sa'=8] {'af','sa'}, dimensions={0} | all-to-all | bytes 262144 | tf_op jit(solution)/shard_map/all_to_all | solution.py:386
  76.0 0.0 copy-done
  76.0 0.0 copy-done.1
  76.0 0.0 copy-done.2
  76.0 0.0 copy-done.3
  76.1 0.0 copy-done.4
  76.1 0.0 copy-done.5
  76.1 0.7 update.1
  (2 shorter events, 0.0 us)
Async XLA Ops:
  23.9 18.0 %all-to-all-start.1 = ((bf16[8,32,256]{2,1,0:T(8,128)(2,1)}), bf16[8,32,256]{2,1,0:T(8,128)(2,1)S(1)}, u32[]{:S(2)}, u32[]{:S(2)}) async-start(bf16[8,32,256]{2,1,0:T(8,128)(2,1)} %join_factors.1), calls=%async_computation.1 | async-start | bytes 262144 | tf_op jit(solution)/shard_map/all_to_all | solution.py:367
  46.9 29.2 %copy-start = (f32[1,2,256]{2,1,0:T(2,128)S(1)}, f32[1,2,256]{2,1,0:T(2,128)}, u32[]{:S(2)}) copy-start(f32[1,2,256]{2,1,0:T(2,128)} %subj_ref.1) | copy-start | bytes 6148
  46.9 29.2 %copy-start.1 = (f32[1,2,256]{2,1,0:T(2,128)S(1)}, f32[1,2,256]{2,1,0:T(2,128)}, u32[]{:S(2)}) copy-start(f32[1,2,256]{2,1,0:T(2,128)} %freq_ref.1) | copy-start | bytes 6148
  46.9 29.2 %copy-start.2 = (f32[1,2,256]{2,1,0:T(2,128)S(1)}, f32[1,2,256]{2,1,0:T(2,128)}, u32[]{:S(2)}) copy-start(f32[1,2,256]{2,1,0:T(2,128)} %time_ref.1) | copy-start | bytes 6148
  46.9 29.2 %copy-start.3 = (f32[1,2,256]{2,1,0:T(2,128)S(1)}, f32[1,2,256]{2,1,0:T(2,128)}, u32[]{:S(2)}) copy-start(f32[1,2,256]{2,1,0:T(2,128)} %time_vel_ref.1) | copy-start | bytes 6148
  46.9 29.2 %copy-start.4 = (f32[1,2,256]{2,1,0:T(2,128)S(1)}, f32[1,2,256]{2,1,0:T(2,128)}, u32[]{:S(2)}) copy-start(f32[1,2,256]{2,1,0:T(2,128)} %freq_vel_ref.1) | copy-start | bytes 6148
  46.9 29.2 %copy-start.5 = (f32[1,2,256]{2,1,0:T(2,128)S(1)}, f32[1,2,256]{2,1,0:T(2,128)}, u32[]{:S(2)}) copy-start(f32[1,2,256]{2,1,0:T(2,128)} %subj_vel_ref.1) | copy-start | bytes 6148
  46.9 11.4 %all-to-all-start.2 = ((bf16[8,32,256]{2,1,0:T(8,128)(2,1)}), bf16[8,32,256]{2,1,0:T(8,128)(2,1)S(1)}, u32[]{:S(2)}, u32[]{:S(2)}) async-start(bf16[8,32,256]{2,1,0:T(8,128)(2,1)} %pair_grads.1), calls=%async_computation.2 | async-start | bytes 262144 | tf_op jit(solution)/shard_map/all_to_all | solution.py:372

commit v6 on v4

--- a/solution.py
+++ b/solution.py
@@ -132,7 +132,7 @@
         b, c = pair_blocks(second_ref, which, which, n_freq)
         grams[which] = gram(b)
         grams[2 + which] = gram(c)
-    step = min(8, bf)
+    step = min(2, bf)
     cap = data_ref.shape[0]
     tables = []
     for slot in range(cap):
@@ -154,8 +154,8 @@
             wide_b, wide_c = b.astype(F32), c.astype(F32)
             freq_data = []
             subj_data = jnp.zeros(wide_c.shape, F32)
-        freq_data.append(jnp.sum(cube * wide_c[None], axis=1))
         for k in range(step):
+            freq_data.append(jnp.sum((cube[k] * wide_c).reshape(bs // 8, 8, -1), axis=0))
             subj_data += cube[k] * wide_b[j + k : j + k + 1]
         if j + step == bf:
             live = slot < where_ref[3, slot]
@@ -163,6 +163,9 @@
             time_gram = time_grams_ref[where_ref[0, slot]]
             freq_grad = model_part(b, time_gram * grams[2 + subj_at])
             subj_grad = model_part(c, time_gram * grams[freq_at])
+            freq_data = [
+                jnp.sum(jnp.stack(freq_data[row : row + 8]), axis=1) for row in range(0, bf, 8)
+            ]
             freq_grad = jnp.where(live, freq_grad - jnp.concatenate(freq_data, axis=0), 0.0)
             subj_grad = jnp.where(live, subj_grad - subj_data, 0.0)
             freq[pl.ds(pl.multiple_of(freq_at * bf, bf), bf), :] += freq_grad

time: 77.2 us -> 77.2 us (level)
  no operation moved by 1% of the time
where the time goes in v6:
time: 77.2 us; the launch traced here: 76.7 us
  blocking collectives  39.4 us (51%)
  starting transfers between devices  13.5 us (17%)
  Pallas kernels  11.3 us (15%)
  waiting for transfers between devices  9.64 us (12%)
  between operations  1.37 us (2%)
    all_to_all x1, blocking collectives, per_device(): first = lax.all_to_all(packed, ('af', 'sa'), 0, 0, tiled=True)  21.8 us
    all_to_all x1, blocking collectives, per_device(): fourth = lax.all_to_all(packed_grads, ('af', 'sa'), 0, 0, tiled=True)  17.7 us
    all_to_all x1, starting transfers between devices, per_device(): second = lax.all_to_all(joined, 'ta', 0, 0, tiled=True)  10 us
    pallas_call x1, Pallas kernels, pair_grads(): kernel_call(functools.partial(pair_body, n_freq), jax.ShapeDtypeStruct(se...  5.04 us
    all_to_all x1, waiting for transfers between devices, per_device(): second = lax.all_to_all(joined, 'ta', 0, 0, tiled=True)  4.83 us
    all_to_all x1, waiting for transfers between devices, per_device(): third = lax.all_to_all(pair, 'ta', 0, 0, tiled=True)  4.81 us
    all_to_all x1, starting transfers between devices, per_device(): third = lax.all_to_all(pair, 'ta', 0, 0, tiled=True)  3.51 us
    pallas_call x1, Pallas kernels, time_grads(): kernel_call(functools.partial(time_body, n_freq), jax.ShapeDtypeStruct((2...  3.02 us
  transfers between devices with their start and end apart: 2, of which 2 were waited for; matrix products, arithmetic and copies ran while one was open for 1% of the time, Pallas kernels for 6%

profile of v6, /device:TPU:1, one launch (start us, length us, event | category | flops | bytes accessed | tf_op | source)
XLA Modules:
  0.0 76.7 jit_solution(10896727587296302508)
XLA Ops:
  0.6 0.7 pad_maximum_fusion.own_ref
  1.4 21.8 %all_to_all.20.got_ref = bf16[64,8,128]{2,1,0:T(8,128)(2,1)S(1)} all-to-all(bf16[64,8,128]{2,1,0:T(8,128)(2,1)S(1)} %pack_factors.1.packed_ref), channel_id=1, replica_groups=mesh['ta'=8,'af'=8,'sa'=8] {'af','sa'}, dimensions={0} | all-to-all | bytes 262144 | tf_op jit(solution)/shard_map/all_to_all | solution.py:349
  23.1 0.7 join_factors.1
  23.8 10.0 %all-to-all-start.1 = ((bf16[8,32,256]{2,1,0:T(8,128)(2,1)}), bf16[8,32,256]{2,1,0:T(8,128)(2,1)S(1)}, u32[]{:S(2)}, u32[]{:S(2)}) async-start(bf16[8,32,256]{2,1,0:T(8,128)(2,1)} %join_factors.1), calls=%async_computation.1 | async-start | bytes 262144 | tf_op jit(solution)/shard_map/all_to_all | solution.py:360
  34.5 0.7 copy.17
  35.2 1.7 %fetch.1 = (bf16[4,64,4096]{2,1,0:T(8,128)(2,1)S(1)}, f32[2,256,256]{2,1,0:T(8,128)S(1)}, bf16[128,256]{1,0:T(8,128)(2,1)S(1)}) custom-call(bf16[1,1,1,4,64,4096]{5,4,3,2,1,0:T(8,128)(2,1)} %blocks_ref.1, bf16[64,8,128]{2,1,0:T(8,128)(2,1)S(1)} %all_to_all.20.got_ref), custom_call_target="tpu_custom_call" | custom-call | flops 4194304 | bytes 20971 | tf_op jit(solution)/shard_map/fetch/pallas_call | solution.py:216
  37.0 4.8 %all-to-all-done.1.second_ref = bf16[8,32,256]{2,1,0:T(8,128)(2,1)S(1)} async-done(((bf16[8,32,256]{2,1,0:T(8,128)(2,1)}), bf16[8,32,256]{2,1,0:T(8,128)(2,1)S(1)}, u32[]{:S(2)}, u32[]{:S(2)}) %all-to-all-start.1) | async-done | bytes 131104 | tf_op jit(solution)/shard_map/all_to_all | solution.py:360
  41.8 5.0 %pair_grads.1 = bf16[8,32,256]{2,1,0:T(8,128)(2,1)} custom-call(s32[4,4]{1,0:T(4,128)S(1)} %concatenate.6.where_ref, bf16[4,64,4096]{2,1,0:T(8,128)(2,1)S(1)} %get-tuple-element.11.data_ref, bf16[128,256]{1,0:T(8,128)(2,1)S(1)} %get-tuple-element.12.time_ref, f32[2,256,256]{2,1,0:T(8,128)S(1)} %get-tuple-element.13.time_grams_ref, ...), custom_call_target="tpu_custom_call" | custom-call | flops 536870912 | bytes 2684354 | tf_op jit(solution)/shard_map/pair_grads/pallas_call | solution.py:237
  46.8 0.0 copy-start
  46.8 0.0 copy-start.1
  46.8 0.0 copy-start.2
  46.8 0.0 copy-start.3
  46.9 0.0 copy-start.4
  46.9 0.0 copy-start.5
  46.9 3.5 %all-to-all-start.2 = ((bf16[8,32,256]{2,1,0:T(8,128)(2,1)}), bf16[8,32,256]{2,1,0:T(8,128)(2,1)S(1)}, u32[]{:S(2)}, u32[]{:S(2)}) async-start(bf16[8,32,256]{2,1,0:T(8,128)(2,1)} %pair_grads.1), calls=%async_computation.2 | async-start | bytes 262144 | tf_op jit(solution)/shard_map/all_to_all | solution.py:365
  50.4 3.0 %time_grads.1.time_ref = f32[2,128,128]{2,1,0:T(8,128)S(1)} custom-call(s32[4,4]{1,0:T(4,128)S(1)} %concatenate.6.where_ref, bf16[4,64,4096]{2,1,0:T(8,128)(2,1)S(1)} %get-tuple-element.11.data_ref, bf16[128,256]{1,0:T(8,128)(2,1)S(1)} %get-tuple-element.12.time_ref, bf16[8,32,256]{2,1,0:T(8,128)(2,1)S(1)} %all-to-all-done.1.second_ref), custom_call_target="tpu_custom_call" | custom-call | flops 536870912 | bytes 2684354 | tf_op jit(solution)/shard_map/time_grads/pallas_call | solution.py:253
  53.4 4.8 %all-to-all-done.2.got_ref = bf16[8,32,256]{2,1,0:T(8,128)(2,1)S(1)} async-done(((bf16[8,32,256]{2,1,0:T(8,128)(2,1)}), bf16[8,32,256]{2,1,0:T(8,128)(2,1)S(1)}, u32[]{:S(2)}, u32[]{:S(2)}) %all-to-all-start.2) | async-done | bytes 131104 | tf_op jit(solution)/shard_map/all_to_all | solution.py:365
  58.2 0.1 pack_grads.1
  58.3 17.7 %all_to_all.21.got_ref = bf16[64,8,128]{2,1,0:T(8,128)(2,1)S(1)} all-to-all(bf16[64,8,128]{2,1,0:T(8,128)(2,1)S(1)} %get-tuple-element.14), channel_id=1, replica_groups=mesh['ta'=8,'af'=8,'sa'=8] {'af','sa'}, dimensions={0} | all-to-all | bytes 262144 | tf_op jit(solution)/shard_map/all_to_all | solution.py:379
  76.0 0.0 copy-done
  76.0 0.0 copy-done.1
  76.0 0.0 copy-done.2
  76.0 0.0 copy-done.3
  76.0 0.0 copy-done.4
  76.0 0.0 copy-done.5
  76.0 0.7 update.1
  (2 shorter events, 0.0 us)
Async XLA Ops:
  23.8 18.0 %all-to-all-start.1 = ((bf16[8,32,256]{2,1,0:T(8,128)(2,1)}), bf16[8,32,256]{2,1,0:T(8,128)(2,1)S(1)}, u32[]{:S(2)}, u32[]{:S(2)}) async-start(bf16[8,32,256]{2,1,0:T(8,128)(2,1)} %join_factors.1), calls=%async_computation.1 | async-start | bytes 262144 | tf_op jit(solution)/shard_map/all_to_all | solution.py:360
  46.8 29.1 %copy-start = (f32[1,2,256]{2,1,0:T(2,128)S(1)}, f32[1,2,256]{2,1,0:T(2,128)}, u32[]{:S(2)}) copy-start(f32[1,2,256]{2,1,0:T(2,128)} %subj_ref.1) | copy-start | bytes 6148
  46.8 29.2 %copy-start.1 = (f32[1,2,256]{2,1,0:T(2,128)S(1)}, f32[1,2,256]{2,1,0:T(2,128)}, u32[]{:S(2)}) copy-start(f32[1,2,256]{2,1,0:T(2,128)} %freq_ref.1) | copy-start | bytes 6148
  46.8 29.2 %copy-start.2 = (f32[1,2,256]{2,1,0:T(2,128)S(1)}, f32[1,2,256]{2,1,0:T(2,128)}, u32[]{:S(2)}) copy-start(f32[1,2,256]{2,1,0:T(2,128)} %time_ref.1) | copy-start | bytes 6148
  46.8 29.2 %copy-start.3 = (f32[1,2,256]{2,1,0:T(2,128)S(1)}, f32[1,2,256]{2,1,0:T(2,128)}, u32[]{:S(2)}) copy-start(f32[1,2,256]{2,1,0:T(2,128)} %time_vel_ref.1) | copy-start | bytes 6148
  46.9 29.2 %copy-start.4 = (f32[1,2,256]{2,1,0:T(2,128)S(1)}, f32[1,2,256]{2,1,0:T(2,128)}, u32[]{:S(2)}) copy-start(f32[1,2,256]{2,1,0:T(2,128)} %freq_vel_ref.1) | copy-start | bytes 6148
  46.9 29.2 %copy-start.5 = (f32[1,2,256]{2,1,0:T(2,128)S(1)}, f32[1,2,256]{2,1,0:T(2,128)}, u32[]{:S(2)}) copy-start(f32[1,2,256]{2,1,0:T(2,128)} %subj_vel_ref.1) | copy-start | bytes 6148
  46.9 11.4 %all-to-all-start.2 = ((bf16[8,32,256]{2,1,0:T(8,128)(2,1)}), bf16[8,32,256]{2,1,0:T(8,128)(2,1)S(1)}, u32[]{:S(2)}, u32[]{:S(2)}) async-start(bf16[8,32,256]{2,1,0:T(8,128)(2,1)} %pair_grads.1), calls=%async_computation.2 | async-start | bytes 262144 | tf_op jit(solution)/shard_map/all_to_all | solution.py:365
